TPU v7x, 32 devices: a whole 2x2x4 slice. The times are simulated.
32 devices in a mesh: dp: 16 (over z, y, core), owner: 2 (over x).
Axes of the slice: x: 2, y: 2, z: 4, core: 2. Of those that a mesh axis runs over, the one named last changes fastest.
Arguments:
- inputs: bfloat16 [2048, 8192], P('dp'), may hold values from -8 to 8
- out_grads: bfloat16 [2048, 1024], P('dp', 'owner'), may hold values from -12 to 12
- weights: float32 [32, 512, 512], P(('dp', 'owner')), may hold values from -0.0625 to 0.0625
- left_stats: float32 [32, 512, 512], P(('dp', 'owner')), as said below
- right_stats: float32 [32, 512, 512], P(('dp', 'owner')), as said below
- left_roots: float32 [32, 512, 512], P(('dp', 'owner')), as said below
- right_roots: float32 [32, 512, 512], P(('dp', 'owner')), as said below
- refresh: int32 [32], P(('dp', 'owner')), may hold values from 0 to 1, as said below
Outputs:
- new_left_stats: float32 [32, 512, 512], P(('dp', 'owner'))
- new_right_stats: float32 [32, 512, 512], P(('dp', 'owner'))
- new_left_roots: float32 [32, 512, 512], P(('dp', 'owner'))
- new_right_roots: float32 [32, 512, 512], P(('dp', 'owner'))
- update: float32 [32, 512, 512], P(('dp', 'owner'))
- queries: bfloat16 [2048, 1024], P('dp', 'owner')
Inputs may be any that keep to these rules, and one draw needn't show every extreme that they name: For every k, refresh[2k] + refresh[2k + 1] is at most 1, and refresh[0] + refresh[1] is 1. `left_stats`: every block is symmetric positive definite. `right_stats`: every block is symmetric positive definite. `left_roots`: every block is symmetric positive definite. `right_roots`: every block is symmetric positive definite.
All inputs are finite; a program needn't handle non-finite values.
Results may differ from a plain program's by a relative error of at most 0.015.
Values may be sent and summed in bfloat16 or wider, within the bound.
A program may use at most 128 MiB of HBM per device.

v0:
```python
import functools
import math

import jax
import jax.numpy as jnp
from jax import lax
from jax.experimental import pallas as pl
from jax.experimental.pallas import tpu as pltpu
from jax.sharding import PartitionSpec as P

BETA = 0.95
DAMPING = 0.0001
BF16 = jnp.bfloat16
F32 = jnp.float32


def dot(a, b, dims=((1,), (0,))):
    return lax.dot_general(a.astype(BF16), b.astype(BF16), (dims, ((), ())), preferred_element_type=F32)


def split(a):
    high = a.astype(BF16)
    return high, (a - high.astype(F32)).astype(BF16)


def dot3(a, b):
    a_high, a_low = split(a)
    b_high, b_low = split(b)
    return dot(a_high, b_high) + (dot(a_high, b_low) + dot(a_low, b_high))


def inverse_root(statistic):
    shape = statistic.shape
    eye = (lax.broadcasted_iota(jnp.int32, shape, 0) == lax.broadcasted_iota(jnp.int32, shape, 1)).astype(F32)
    damped = statistic + DAMPING * eye
    z = 2.5 / jnp.sqrt(jnp.sum(damped * damped, keepdims=True))
    m = z * damped
    p = dot(m, m)
    r = 1.5625 * m - 0.625 * p + 0.0625 * dot(p, m)
    w = 0.0625 * r + 0.1953125 * m - 0.01953125 * p
    return jnp.sqrt(jnp.sqrt(z)) * (1.5625 * eye - 0.3125 * m - 0.48828125 * r + dot(w, r))


def roots(left_stat, right_stat, left_old, right_old):
    return (inverse_root(left_stat), inverse_root(right_stat))


def stale(left_stat, right_stat, left_old, right_old):
    return (left_old, right_old)

LINE = 4


def flip(index, stride):
    return index + stride - 2 * stride * lax.rem(lax.div(index, stride), 2)


def remote(src, dst, send, recv, peer):
    return pltpu.make_async_remote_copy(
        src_ref=src, dst_ref=dst, send_sem=send, recv_sem=recv,
        device_id=peer, device_id_type=pl.DeviceIdType.MESH,
    )


def greet(peers):
    barrier = pltpu.get_barrier_semaphore()
    for peer in peers:
        pl.semaphore_signal(barrier, inc=1, device_id=peer, device_id_type=pl.DeviceIdType.MESH)
    pl.semaphore_wait(barrier, len(peers))


def by_distance(n):
    return sorted(range(1, n), key=lambda k: -min(k, n - k))


def gather_kernel(n, x_ref, g_ref, f_ref, ga_ref, x_own, g_own, own, fs, fr, xs, xr, zs, zr, ys, yr, cs, cr):
    me, mine = lax.axis_index("dp"), lax.axis_index("owner")
    nz = n // LINE
    rows, width = g_ref.shape
    half = rows // 2
    near = pl.ds(pl.multiple_of(mine * half, half), half)
    far = pl.ds(pl.multiple_of((1 - mine) * half, half), half)
    pair, row = flip(me, 1), flip(me, 2)

    def cols(block):
        return pl.ds(pl.multiple_of(block * width, width), width)

    own_in = [
        pltpu.make_async_copy(x_ref.at[:, cols(me)], x_own, own.at[0]),
        pltpu.make_async_copy(g_ref, g_own, own.at[1]),
    ]
    for copy in own_in:
        copy.start()
    greet([(lax.rem(me + k, n), mine) for k in range(1, n)] + [(me, 1 - mine)])
    sent = []

    def go(copy):
        copy.start()
        sent.append(copy)
        return copy

    z_copy = {}
    for k in by_distance(nz):
        z_copy[k] = go(remote(g_ref, ga_ref.at[me], zs.at[k], zr.at[k], (lax.rem(me + LINE * k, n), mine)))
    f_copy = {}
    order = by_distance(n)
    for k in order:
        peer = lax.rem(me + k, n)
        f_copy[k] = go(remote(x_ref.at[near, cols(peer)], f_ref.at[me, near], fs.at[k], fr.at[k], (peer, mine)))
    y_copy, c_copy = {}, {}
    for k in [0] + by_distance(nz):
        source = lax.rem(me - LINE * k + n, n)
        if k:
            z_copy[k].wait_recv()
        block = ga_ref.at[source] if k else g_ref
        y_copy[k] = go(remote(block, ga_ref.at[source], ys.at[k], yr.at[k], (row, mine)))
        c_copy[k] = go(remote(block, ga_ref.at[source], cs.at[k], cr.at[k], (pair, mine)))
    own_out = [
        pltpu.make_async_copy(x_own, f_ref.at[me], own.at[2]),
        pltpu.make_async_copy(g_own, ga_ref.at[me], own.at[3]),
    ]
    for first, second in zip(own_in, own_out):
        first.wait()
        second.start()
    x_copy = {}

    def pass_on(k):
        f_copy[k].wait_recv()
        held = f_ref.at[lax.rem(me - k + n, n), near]
        x_copy[k] = go(remote(held, held, xs.at[k], xr.at[k], (me, 1 - mine)))

    quick = order[::-1]
    for at, k in enumerate([0] + by_distance(nz)):
        y_copy[k].wait_recv()
        source = lax.rem(row - LINE * k + n, n)
        block = ga_ref.at[source]
        c_copy[nz + k] = go(remote(block, block, cs.at[nz + k], cr.at[nz + k], (pair, mine)))
    for k in quick:
        pass_on(k)
    for k in range(2 * nz):
        c_copy[k].wait_recv()
    for k in quick:
        x_copy[k].wait_recv()
    for copy in own_out:
        copy.wait()
    for copy in sent:
        copy.wait_send()


def gather(n, inputs, out_grads):
    rows, width = out_grads.shape
    nz = n // LINE
    dma = pltpu.SemaphoreType.DMA
    anywhere = pl.BlockSpec(memory_space=pl.ANY)
    return pl.pallas_call(
        functools.partial(gather_kernel, n),
        out_shape=[jax.ShapeDtypeStruct((n, rows, width), BF16)] * 2,
        in_specs=[anywhere] * 2,
        out_specs=[anywhere] * 2,
        scratch_shapes=[pltpu.VMEM((rows, width), BF16)] * 2
        + [dma((4,))] + [dma((n,))] * 4 + [dma((nz,))] * 4 + [dma((2 * nz,))] * 2,
        compiler_params=pltpu.CompilerParams(collective_id=0, has_side_effects=True),
        name="gather_blocks",
    )(inputs, out_grads)


def reduce_kernel(n, f_ref, w_ref, q_ref, a_out, a_in, b_out, b_in, c_out, c_in, total, a_s, a_r, b_s, b_r, c_s, c_r):
    me, mine = lax.axis_index("dp"), lax.axis_index("owner")
    nz = n // LINE
    pair, row = flip(me, 1), flip(me, 2)
    order = by_distance(nz) + [0]
    greet([(pair, mine), (row, mine)] + [(lax.rem(me + LINE * k, n), mine) for k in range(1, nz)])

    def part(block):
        return jnp.dot(f_ref[block], w_ref[...], preferred_element_type=F32)

    sent = []

    def go(copy):
        copy.start()
        sent.append(copy)
        return copy

    a_copy, b_copy, c_copy = {}, {}, {}
    for k in order:
        for turn, base in ((1, flip(row, 1)), (0, pair)):
            at = 2 * k + turn
            a_out[at] = part(lax.rem(base + LINE * k, n)).astype(BF16)
            a_copy[at] = go(remote(a_out.at[at], a_in.at[at], a_s.at[at], a_r.at[at], (pair, mine)))
    for k in order:
        mine_part = part(lax.rem(row + LINE * k, n))
        a_copy[2 * k + 1].wait_recv()
        b_out[k] = (mine_part + a_in[2 * k + 1].astype(F32)).astype(BF16)
        b_copy[k] = go(remote(b_out.at[k], b_in.at[k], b_s.at[k], b_r.at[k], (row, mine)))
    for k in order:
        total[k] = part(lax.rem(me + LINE * k, n))
        a_copy[2 * k].wait_recv()
        total[k] += a_in[2 * k].astype(F32)
    for k in order:
        b_copy[k].wait_recv()
        if k:
            c_out[k] = (total[k] + b_in[k].astype(F32)).astype(BF16)
            peer = lax.rem(me + LINE * k, n)
            c_copy[k] = go(remote(c_out.at[k], c_in.at[k], c_s.at[k], c_r.at[k], (peer, mine)))
    result = total[0] + b_in[0].astype(F32)
    for k in by_distance(nz)[::-1]:
        c_copy[k].wait_recv()
        result = result + c_in[k].astype(F32)
    q_ref[...] = result.astype(BF16)
    for copy in sent:
        copy.wait_send()


def reduce_queries(n, features, updated):
    rows, width = features.shape[1], updated.shape[1]
    nz = n // LINE
    dma = pltpu.SemaphoreType.DMA
    vmem = pl.BlockSpec(memory_space=pltpu.VMEM)
    return pl.pallas_call(
        functools.partial(reduce_kernel, n),
        out_shape=jax.ShapeDtypeStruct((rows, width), BF16),
        in_specs=[vmem] * 2,
        out_specs=vmem,
        scratch_shapes=[pltpu.VMEM((2 * nz, rows, width), BF16)] * 2
        + [pltpu.VMEM((nz, rows, width), BF16)] * 4
        + [pltpu.VMEM((nz, rows, width), F32)]
        + [dma((2 * nz,))] * 2 + [dma((nz,))] * 4,
        compiler_params=pltpu.CompilerParams(collective_id=1, has_side_effects=True),
        name="reduce_queries",
    )(features, updated)


def step_kernel(chunks, tok_total, rate, flag, f_hbm, g_hbm, w_hbm, ls_hbm, rs_hbm, lr_hbm, rr_hbm,
                ls_out, rs_out, lr_out, rr_out, d_out, u_ref,
                f, g, w, ls, rs, lr, rr, d, grad, f_sem, g_sem, in_sem, out_sem):
    span = f.shape[0] // chunks
    pieces = []
    for k in range(chunks):
        part = pl.ds(k * span, span)
        pieces.append((
            pltpu.make_async_copy(f_hbm.at[part], f.at[part], f_sem.at[k]),
            pltpu.make_async_copy(g_hbm.at[part], g.at[part], g_sem.at[k]),
        ))
        for copy in pieces[-1]:
            copy.start()
    ins = [
        pltpu.make_async_copy(src.at[0], dst, in_sem.at[k])
        for k, (src, dst) in enumerate(((ls_hbm, ls), (rs_hbm, rs), (lr_hbm, lr), (rr_hbm, rr), (w_hbm, w)))
    ]
    for copy in ins:
        copy.start()
    outs = [
        pltpu.make_async_copy(src, dst.at[0], out_sem.at[k])
        for k, (src, dst) in enumerate(((ls, ls_out), (rs, rs_out), (lr, lr_out), (rr, rr_out), (d, d_out)))
    ]
    for k, pair in enumerate(pieces):
        for copy in pair:
            copy.wait()
        part = pl.ds(k * span, span)
        term = dot(f[part], g[part], ((0,), (0,))) * (1.0 / tok_total)
        grad[...] = term if k == 0 else grad[...] + term
    high = grad[...].astype(BF16)
    ins[0].wait()
    ls[...] = BETA * ls[...] + (1.0 - BETA) * dot(high, high, ((1,), (1,)))
    outs[0].start()
    ins[1].wait()
    rs[...] = BETA * rs[...] + (1.0 - BETA) * dot(high, high, ((0,), (0,)))
    outs[1].start()
    ins[2].wait()
    ins[3].wait()

    @pl.when(flag[0] > 0)
    def _():
        lr[...] = inverse_root(ls[...])
        rr[...] = inverse_root(rs[...])

    outs[2].start()
    outs[3].start()
    direction = dot3(dot3(lr[...], grad[...]), rr[...])
    norm = jnp.sqrt(jnp.sum(direction * direction, keepdims=True) + 1e-12)
    direction = direction * (direction.shape[0] / norm)
    d[...] = direction
    outs[4].start()
    ins[4].wait()
    u_ref[...] = (w[...] - rate * direction).astype(BF16)
    for copy in outs:
        copy.wait()


def owner_step(tok_total, rate, features, grads, weights, left_stats, right_stats, left_roots, right_roots, refresh):
    block = weights.shape[1]
    chunks = 4
    dma = pltpu.SemaphoreType.DMA
    anywhere = pl.BlockSpec(memory_space=pl.ANY)
    square = pltpu.VMEM((block, block), F32)
    return pl.pallas_call(
        functools.partial(step_kernel, chunks, tok_total, rate),
        out_shape=[jax.ShapeDtypeStruct((1, block, block), F32)] * 5 + [jax.ShapeDtypeStruct((block, block), BF16)],
        in_specs=[pl.BlockSpec(memory_space=pltpu.SMEM)] + [anywhere] * 7,
        out_specs=[anywhere] * 5 + [pl.BlockSpec(memory_space=pltpu.VMEM)],
        scratch_shapes=[pltpu.VMEM(features.shape, BF16)] * 2 + [square] * 7
        + [dma((chunks,))] * 2 + [dma((5,))] * 2,
        compiler_params=pltpu.CompilerParams(vmem_limit_bytes=56 << 20),
        name="owner_step",
    )(refresh, features, grads, weights, left_stats, right_stats, left_roots, right_roots)


def body(inputs, out_grads, weights, left_stats, right_stats, left_roots, right_roots, refresh):
    tok_local, model_width = inputs.shape
    block = weights.shape[1]
    col_count = out_grads.shape[1]
    row_blocks = model_width // block
    col_blocks = col_count // block
    replicas = lax.axis_size("dp")
    tok_total = tok_local * replicas
    kernels = col_blocks == 1 and lax.axis_size("owner") == 2 and replicas % LINE == 0
    rate = 0.25 / math.sqrt(model_width)
    if kernels:
        features, grads = gather(replicas, inputs, out_grads)
        outs = owner_step(
            tok_total, rate, features.reshape(tok_total, block), grads.reshape(tok_total, block),
            weights, left_stats, right_stats, left_roots, right_roots, refresh,
        )
        return (*outs[:5], reduce_queries(replicas, features, outs[5]))
    mine = lax.axis_index("dp") % col_blocks
    grads = lax.all_gather(out_grads, "dp", axis=0, tiled=True)
    grads = lax.dynamic_slice_in_dim(grads, mine * block, block, 1)
    send = jnp.repeat(inputs.reshape(tok_local, row_blocks, block).transpose(1, 0, 2), col_blocks, axis=0)
    features = lax.all_to_all(send, "dp", split_axis=0, concat_axis=0, tiled=True)
    features = features.reshape(tok_total, block)
    gradient = dot(features, grads, ((0,), (0,))) / tok_total
    left_new = BETA * left_stats[0] + (1.0 - BETA) * dot(gradient, gradient, ((1,), (1,)))
    right_new = BETA * right_stats[0] + (1.0 - BETA) * dot(gradient, gradient, ((0,), (0,)))
    left_root, right_root = lax.cond(
        refresh[0] > 0, roots, stale, left_new, right_new, left_roots[0], right_roots[0]
    )
    direction = dot3(dot3(left_root, gradient), right_root)
    direction = direction * (block / jnp.sqrt(jnp.sum(direction * direction) + 1e-12))
    updated = (weights[0] - rate * direction).astype(BF16)
    partial = dot(features, updated).astype(BF16)
    if col_blocks > 1:
        partial = lax.dynamic_update_slice(jnp.zeros((tok_total, col_count), BF16), partial, (0, mine * block))
    queries = lax.psum_scatter(partial, "dp", scatter_dimension=0, tiled=True)
    return (left_new[None], right_new[None], left_root[None], right_root[None], direction[None], queries)


def solution(mesh):
    blocks = P(("dp", "owner"), None, None)
    in_specs = (P("dp", None), P("dp", "owner"), blocks, blocks, blocks, blocks, blocks, P(("dp", "owner")))
    out_specs = (blocks,) * 5 + (P("dp", "owner"),)
    return jax.shard_map(body, mesh=mesh, in_specs=in_specs, out_specs=out_specs, check_vma=False)
```

profile of v0, /device:TPU:0, one launch (start us, length us, event | category | flops | bytes accessed | tf_op | source)
XLA Modules:
  0.0 100.2 jit_solution(8225617456803285436)
XLA Ops:
  1.3 52.9 %gather_blocks.1 = (bf16[16,128,512]{2,1,0:T(8,128)(2,1)}, bf16[16,128,512]{2,1,0:T(8,128)(2,1)}) custom-call(bf16[128,8192]{1,0:T(8,128)(2,1)} %x_ref.1, bf16[128,512]{1,0:T(8,128)(2,1)} %g_ref.1), custom_call_target="tpu_custom_call" | custom-call | tf_op jit(solution)/shard_map/gather_blocks/pallas_call | solution.py:155
  54.1 12.0 %owner_step.1 = (f32[1,512,512]{2,1,0:T(8,128)}, f32[1,512,512]{2,1,0:T(8,128)}, f32[1,512,512]{2,1,0:T(8,128)}, f32[1,512,512]{2,1,0:T(8,128)}, f32[1,512,512]{2,1,0:T(8,128)}, /*index=5*/bf16[512,512]{1,0:T(8,128)(2,1)}) custom-call(s32[1]{0:T(128)S(6)} %copy.15.flag, bf16[2048,512]{1,0:T(8,128)(2,1)} %bitcast.2, bf16[2048,512]{1,0:T(8,128)(2,1)} %bitcast.3, ...), custom_call_target="tpu_custom_call" | custom-call | tf_op jit(solution)/shard_map/owner_step/pallas_call | solution.py:296
  66.1 32.5 %reduce_queries.1 = bf16[128,512]{1,0:T(8,128)(2,1)} custom-call(bf16[16,128,512]{2,1,0:T(8,128)(2,1)} %get-tuple-element.14.f_ref, bf16[512,512]{1,0:T(8,128)(2,1)} %get-tuple-element.21.w_ref), custom_call_target="tpu_custom_call" | custom-call | tf_op jit(solution)/shard_map/reduce_queries/pallas_call | solution.py:219
  98.6 1.6 %copy.16 = bf16[128,512]{1,0:T(8,128)(2,1)} copy(bf16[128,512]{1,0:T(8,128)(2,1)} %reduce_queries.1) | data formatting | bytes 262144
where the time goes:
time: 101 us; the launch traced here: 100 us
  Pallas kernels  97.3 us (96%)
  local copies, waits for them, and re-layouts  1.57 us (2%)
  between operations  1.3 us (1%)
    pallas_call x1, Pallas kernels, gather(): pl.pallas_call(functools.partial(gather_kernel, n), out_shape=[jax.ShapeD...  52.9 us
    pallas_call x1, Pallas kernels, reduce_queries(): pl.pallas_call(functools.partial(reduce_kernel, n), out_shape=jax.ShapeDt...  32.5 us
    pallas_call x1, Pallas kernels, owner_step(): pl.pallas_call(functools.partial(step_kernel, chunks, tok_total, rate), o...  12 us

commit v1 on v0

v1 whole, which is shorter than its diff:
```python
import functools
import math

import jax
import jax.numpy as jnp
from jax import lax
from jax.experimental import pallas as pl
from jax.experimental.pallas import tpu as pltpu
from jax.sharding import PartitionSpec as P

BETA = 0.95
DAMPING = 0.0001
BF16 = jnp.bfloat16
F32 = jnp.float32


def dot(a, b, dims=((1,), (0,))):
    return lax.dot_general(a.astype(BF16), b.astype(BF16), (dims, ((), ())), preferred_element_type=F32)


def split(a):
    high = a.astype(BF16)
    return high, (a - high.astype(F32)).astype(BF16)


def dot3(a, b):
    a_high, a_low = split(a)
    b_high, b_low = split(b)
    return dot(a_high, b_high) + (dot(a_high, b_low) + dot(a_low, b_high))


def inverse_root(statistic):
    shape = statistic.shape
    eye = (lax.broadcasted_iota(jnp.int32, shape, 0) == lax.broadcasted_iota(jnp.int32, shape, 1)).astype(F32)
    damped = statistic + DAMPING * eye
    z = 2.5 / jnp.sqrt(jnp.sum(damped * damped, keepdims=True))
    m = z * damped
    p = dot(m, m)
    r = 1.5625 * m - 0.625 * p + 0.0625 * dot(p, m)
    w = 0.0625 * r + 0.1953125 * m - 0.01953125 * p
    return jnp.sqrt(jnp.sqrt(z)) * (1.5625 * eye - 0.3125 * m - 0.48828125 * r + dot(w, r))


def roots(left_stat, right_stat, left_old, right_old):
    return (inverse_root(left_stat), inverse_root(right_stat))


def stale(left_stat, right_stat, left_old, right_old):
    return (left_old, right_old)

LINE = 4


def flip(index, stride):
    return index + stride - 2 * stride * lax.rem(lax.div(index, stride), 2)


def remote(src, dst, send, recv, peer):
    return pltpu.make_async_remote_copy(
        src_ref=src, dst_ref=dst, send_sem=send, recv_sem=recv,
        device_id=peer, device_id_type=pl.DeviceIdType.MESH,
    )


def greet(peers):
    barrier = pltpu.get_barrier_semaphore()
    for peer in peers:
        pl.semaphore_signal(barrier, inc=1, device_id=peer, device_id_type=pl.DeviceIdType.MESH)
    pl.semaphore_wait(barrier, len(peers))


def toggle(index, bits):
    stride = 1
    while stride <= bits:
        if bits & stride:
            index = flip(index, stride)
        stride *= 2
    return index


ORDER = (
    "g", "x1", "x10", "x2", "x14", "x3", "x4", "h", "x6", "x11", "x15", "x5", "x8", "x7", "x12", "x9",
    "x13", "i1", "p1", "p2", "p4", "p10", "y0", "p3", "i3", "p14", "p6", "p11", "y2", "p15", "d0", "p5",
    "p7", "y1", "d2", "p8", "p12", "d10", "p9", "p13", "y3", "d14", "s3", "s11", "s15", "d6", "s7", "d4",
    "s5", "d8", "s9", "d12", "s13",
)


class Copies:
    def __init__(self):
        self.sent = []

    def go(self, src, dst, send, recv, peer):
        copy = remote(src, dst, send, recv, peer)
        copy.start()
        self.sent.append(copy)
        return copy

    def drain(self):
        for copy in self.sent:
            copy.wait_send()


def gather_phase(n, copies, x_ref, g_ref, f, fs, ga, grad, own, x_s, x_r, p_s, p_r, z_s, z_r, y_s, y_r, c_s, c_r, s_s, s_r):
    me, mine = lax.axis_index("dp"), lax.axis_index("owner")
    rows, width = g_ref.shape
    half = rows // 2
    near = pl.ds(pl.multiple_of(mine * half, half), half)
    pair, row = flip(me, 1), flip(me, 2)
    go = copies.go

    def cols(block):
        return pl.ds(pl.multiple_of(block * width, width), width)

    own_in = [
        pltpu.make_async_copy(x_ref.at[:, cols(me)], f.at[me], own.at[0]),
        pltpu.make_async_copy(g_ref, ga.at[me], own.at[1]),
        pltpu.make_async_copy(x_ref.at[:, cols(pair)], fs.at[lax.div(me, 2)], own.at[2]),
    ]
    x_copy, p_copy, z_copy, y_copy, c_copy, s_copy = {}, {}, {}, {}, {}, {}

    def fan(t, block):
        slot = toggle(me, LINE * t)
        y_copy[t] = go(block, ga.at[slot], y_s.at[t], y_r.at[t], (row, mine))
        c_copy[t] = go(block, ga.at[slot], c_s.at[t], c_r.at[t], (pair, mine))

    def g(_):
        for copy in own_in:
            copy.start()
        for t in (2, 1):
            z_copy[t] = go(g_ref, ga.at[me], z_s.at[t], z_r.at[t], (toggle(me, LINE * t), mine))
        fan(0, g_ref)

    def h(_):
        z_copy[2].wait_recv()
        held = ga.at[toggle(me, LINE * 2)]
        z_copy[3] = go(held, held, z_s.at[3], z_r.at[3], (toggle(me, LINE), mine))
        fan(2, held)

    def i(t):
        z_copy[t].wait_recv()
        fan(t, ga.at[toggle(me, LINE * t)])

    def y(t):
        y_copy[t].wait_recv()
        held = ga.at[toggle(row, LINE * t)]
        c_copy[LINE + t] = go(held, held, c_s.at[LINE + t], c_r.at[LINE + t], (pair, mine))

    def x(k):
        peer = toggle(me, k)
        if k == 1:
            src, dst = x_ref.at[:, cols(peer)], f.at[me]
        else:
            src, dst = x_ref.at[near, cols(peer)], f.at[me, near]
        x_copy[k] = go(src, dst, x_s.at[k], x_r.at[k], (peer, mine))

    def p(k):
        x_copy[k].wait_recv()
        if k > 1:
            held = f.at[toggle(me, k), near]
            p_copy[k] = go(held, held, p_s.at[k], p_r.at[k], (me, 1 - mine))

    def d(k):
        for at in (k, k + 1):
            if at > 1:
                p_copy[at].wait_recv()
        if k == 0:
            own_in[0].wait()
            own_in[1].wait()
        t = k // LINE
        c_copy[t + LINE if k % LINE else t].wait_recv()
        chip = pl.multiple_of(2 * lax.div(toggle(me, k), 2), 2)
        term = dot(
            f[pl.ds(chip, 2)].reshape(2 * rows, width), ga[pl.ds(chip, 2)].reshape(2 * rows, width), ((0,), (0,))
        )
        grad[...] = term if k == 0 else grad[...] + term

    def s(k):
        source = toggle(me, k)
        s_copy[k] = go(f.at[source], fs.at[lax.div(source, 2)], s_s.at[k], s_r.at[k], (pair, mine))

    steps = dict(g=g, h=h, i=i, y=y, x=x, p=p, d=d, s=s)
    for word in ORDER:
        steps[word[0]](int(word[1:] or 0))
    return own_in[2], s_copy


def reduce_phase(n, copies, f, fs, u, us, arrived, tot, a_out, a_in, b_out, b_in, a_s, a_r, b_s, b_r, u_copy, q_ref):
    me, mine = lax.axis_index("dp"), lax.axis_index("owner")
    row = flip(me, 2)
    rows = q_ref.shape[0]
    half = rows // 2
    go = copies.go
    halves = [pl.ds(k * half, half) for k in range(2)]

    def near_part(base, t):
        return dot(f[toggle(base, LINE * t)], u[...])

    def far_part(base, t):
        return dot(fs[lax.div(toggle(base, LINE * t), 2)], us[...])

    a_copy, b_copy = {}, {}
    ahead = near_part(row, 3)
    for copy in arrived:
        copy.wait()
    for copy in u_copy:
        copy.wait_recv()
    for t in (3, 2, 1, 0):
        a_out[t] = ((ahead if t == 3 else near_part(row, t)) + far_part(row, t)).astype(BF16)
        for k in range(2):
            a_copy[t, k] = go(a_out.at[t, halves[k]], a_in.at[t, halves[k]], a_s.at[2 * t + k], a_r.at[2 * t + k], (row, mine))

    def total(t):
        tot[t] = near_part(me, t) + far_part(me, t)

    def pass_on(t, k, peer, extra=None):
        a_copy[t, k].wait_recv()
        value = tot[t, halves[k]] + a_in[t, halves[k]].astype(F32)
        if extra is not None:
            b_copy[extra, k].wait_recv()
            value = value + b_in[extra, halves[k]].astype(F32)
        b_out[t, halves[k]] = value.astype(BF16)
        b_copy[t, k] = go(b_out.at[t, halves[k]], b_in.at[t, halves[k]], b_s.at[2 * t + k], b_r.at[2 * t + k], (peer, mine))

    total(3)
    for k in range(2):
        pass_on(3, k, toggle(me, LINE))
    total(2)
    total(1)
    total(0)
    for k in range(2):
        pass_on(2, k, toggle(me, 2 * LINE), 3)
    for k in range(2):
        pass_on(1, k, toggle(me, LINE))
    for k in range(2):
        a_copy[0, k].wait_recv()
        value = tot[0, halves[k]] + a_in[0, halves[k]].astype(F32)
        b_copy[2, k].wait_recv()
        value = value + b_in[2, halves[k]].astype(F32)
        b_copy[1, k].wait_recv()
        q_ref[halves[k]] = (value + b_in[1, halves[k]].astype(F32)).astype(BF16)


def step_kernel(n, rate, flag, x_ref, g_ref, w_hbm, ls_hbm, rs_hbm, lr_hbm, rr_hbm,
                ls_out, rs_out, lr_out, rr_out, d_out, q_ref,
                f, fs, ga, grad, w, ls, rs, lr, rr, d, u, us, tot, a_out, a_in, b_out, b_in,
                in_sem, out_sem, own, x_s, x_r, p_s, p_r, z_s, z_r, y_s, y_r, c_s, c_r, s_s, s_r, u_s, u_r, a_s, a_r, b_s, b_r):
    me, mine = lax.axis_index("dp"), lax.axis_index("owner")
    pair = flip(me, 1)
    block = w.shape[0]
    greet([(toggle(me, k), mine) for k in range(1, n)] + [(me, 1 - mine)])
    copies = Copies()
    ins = [
        pltpu.make_async_copy(src.at[0], dst, in_sem.at[k])
        for k, (src, dst) in enumerate(((ls_hbm, ls), (rs_hbm, rs), (lr_hbm, lr), (rr_hbm, rr), (w_hbm, w)))
    ]
    for copy in ins:
        copy.start()
    own_side, s_copy = gather_phase(
        n, copies, x_ref, g_ref, f, fs, ga, grad, own, x_s, x_r, p_s, p_r, z_s, z_r, y_s, y_r, c_s, c_r, s_s, s_r
    )
    outs = [
        pltpu.make_async_copy(src, dst.at[0], out_sem.at[k])
        for k, (src, dst) in enumerate(((ls, ls_out), (rs, rs_out), (lr, lr_out), (rr, rr_out), (d, d_out)))
    ]
    grad[...] = grad[...] * (1.0 / (n * g_ref.shape[0]))
    high = grad[...].astype(BF16)
    for copy in ins:
        copy.wait()
    ls[...] = BETA * ls[...] + (1.0 - BETA) * dot(high, high, ((1,), (1,)))
    outs[0].start()
    rs[...] = BETA * rs[...] + (1.0 - BETA) * dot(high, high, ((0,), (0,)))
    outs[1].start()
    anew = jnp.full((block, block), flag[0], jnp.int32) > 0
    lr[...] = jnp.where(anew, inverse_root(ls[...]), lr[...])
    outs[2].start()
    rr[...] = jnp.where(anew, inverse_root(rs[...]), rr[...])
    outs[3].start()
    direction = dot3(dot3(lr[...], grad[...]), rr[...])
    norm = jnp.sqrt(jnp.sum(direction * direction, keepdims=True) + 1e-12)
    direction = direction * (block / norm)
    d[...] = direction
    outs[4].start()
    u[...] = (w[...] - rate * direction).astype(BF16)
    u_copy = [copies.go(u, us, u_s.at[0], u_r.at[0], (pair, mine))]
    for copy in s_copy.values():
        copy.wait_recv()
    reduce_phase(n, copies, f, fs, u, us, [own_side], tot, a_out, a_in, b_out, b_in, a_s, a_r, b_s, b_r, u_copy, q_ref)
    for copy in outs:
        copy.wait()
    copies.drain()


def fused_step(n, rate, inputs, out_grads, weights, left_stats, right_stats, left_roots, right_roots, refresh):
    rows, width = out_grads.shape
    block = weights.shape[1]
    nz = n // LINE
    dma = pltpu.SemaphoreType.DMA
    anywhere = pl.BlockSpec(memory_space=pl.ANY)
    square = pltpu.VMEM((block, block), F32)
    narrow = pltpu.VMEM((block, block), BF16)
    shards = pltpu.VMEM((nz, rows, width), BF16)
    return pl.pallas_call(
        functools.partial(step_kernel, n, rate),
        out_shape=[jax.ShapeDtypeStruct((1, block, block), F32)] * 5 + [jax.ShapeDtypeStruct((rows, width), BF16)],
        in_specs=[pl.BlockSpec(memory_space=pltpu.SMEM)] + [anywhere] * 7,
        out_specs=[anywhere] * 5 + [pl.BlockSpec(memory_space=pltpu.VMEM)],
        scratch_shapes=[
            pltpu.VMEM((n, rows, block), BF16), pltpu.VMEM((n // 2, rows, block), BF16), pltpu.VMEM((n, rows, width), BF16),
        ] + [square] * 7 + [narrow] * 2 + [pltpu.VMEM((nz, rows, width), F32)] + [shards] * 4
        + [dma((5,))] * 2 + [dma((3,))] + [dma((n,))] * 4 + [dma((LINE,))] * 4 + [dma((2 * LINE,))] * 2 + [dma((n,))] * 2
        + [dma((1,))] * 2 + [dma((2 * LINE,))] * 4,
        compiler_params=pltpu.CompilerParams(collective_id=0, has_side_effects=True, vmem_limit_bytes=48 << 20),
        name="fused_step",
    )(refresh, inputs, out_grads, weights, left_stats, right_stats, left_roots, right_roots)


def body(inputs, out_grads, weights, left_stats, right_stats, left_roots, right_roots, refresh):
    tok_local, model_width = inputs.shape
    block = weights.shape[1]
    col_count = out_grads.shape[1]
    row_blocks = model_width // block
    col_blocks = col_count // block
    replicas = lax.axis_size("dp")
    tok_total = tok_local * replicas
    kernels = col_blocks == 1 and lax.axis_size("owner") == 2 and replicas == 4 * LINE
    rate = 0.25 / math.sqrt(model_width)
    if kernels:
        return fused_step(
            replicas, rate, inputs, out_grads, weights, left_stats, right_stats, left_roots, right_roots, refresh
        )
    mine = lax.axis_index("dp") % col_blocks
    grads = lax.all_gather(out_grads, "dp", axis=0, tiled=True)
    grads = lax.dynamic_slice_in_dim(grads, mine * block, block, 1)
    send = jnp.repeat(inputs.reshape(tok_local, row_blocks, block).transpose(1, 0, 2), col_blocks, axis=0)
    features = lax.all_to_all(send, "dp", split_axis=0, concat_axis=0, tiled=True)
    features = features.reshape(tok_total, block)
    gradient = dot(features, grads, ((0,), (0,))) / tok_total
    left_new = BETA * left_stats[0] + (1.0 - BETA) * dot(gradient, gradient, ((1,), (1,)))
    right_new = BETA * right_stats[0] + (1.0 - BETA) * dot(gradient, gradient, ((0,), (0,)))
    left_root, right_root = lax.cond(
        refresh[0] > 0, roots, stale, left_new, right_new, left_roots[0], right_roots[0]
    )
    direction = dot3(dot3(left_root, gradient), right_root)
    direction = direction * (block / jnp.sqrt(jnp.sum(direction * direction) + 1e-12))
    updated = (weights[0] - rate * direction).astype(BF16)
    partial = dot(features, updated).astype(BF16)
    if col_blocks > 1:
        partial = lax.dynamic_update_slice(jnp.zeros((tok_total, col_count), BF16), partial, (0, mine * block))
    queries = lax.psum_scatter(partial, "dp", scatter_dimension=0, tiled=True)
    return (left_new[None], right_new[None], left_root[None], right_root[None], direction[None], queries)


def solution(mesh):
    blocks = P(("dp", "owner"), None, None)
    in_specs = (P("dp", None), P("dp", "owner"), blocks, blocks, blocks, blocks, blocks, P(("dp", "owner")))
    out_specs = (blocks,) * 5 + (P("dp", "owner"),)
    return jax.shard_map(body, mesh=mesh, in_specs=in_specs, out_specs=out_specs, check_vma=False)
```

time: 101 us -> 73.6 us (0.73)
  Pallas kernels: 97.3 us -> 65.7 us
  local copies, waits for them, and re-layouts: 1.57 us -> 6.4 us
    pallas_call x3 -> x1, Pallas kernels: 97.3 us -> 65.7 us  [fused_step(): pl.pallas_call(functools.partial(step_kernel, n, rate), out_shape=[jax.Sh...]
    unnamed x1 -> x8, local copies, waits for them, and re-layouts: 1.57 us -> 6.4 us
where the time goes in v1:
time: 73.6 us; the launch traced here: 73.4 us
  Pallas kernels  65.7 us (89%)
  local copies, waits for them, and re-layouts  6.4 us (9%)
  between operations  1.3 us (2%)
    pallas_call x1, Pallas kernels, fused_step(): pl.pallas_call(functools.partial(step_kernel, n, rate), out_shape=[jax.Sh...  65.7 us
    unnamed x8, local copies, waits for them, and re-layouts  6.4 us

profile of v1, /device:TPU:0, one launch (start us, length us, event | category | flops | bytes accessed | tf_op | source)
XLA Modules:
  0.0 73.4 jit_solution(10081324449720253171)
XLA Ops:
  1.3 0.0 copy-start
  1.3 0.9 %copy-done = bf16[128,512]{1,0:T(8,128)(2,1)S(1)} copy-done((bf16[128,512]{1,0:T(8,128)(2,1)S(1)}, bf16[128,512]{1,0:T(8,128)(2,1)}, u32[]{:S(2)}) %copy-start) | copy-done | bytes 131096
  2.2 65.7 %fused_step.1 = (f32[1,512,512]{2,1,0:T(8,128)S(1)}, f32[1,512,512]{2,1,0:T(8,128)S(1)}, f32[1,512,512]{2,1,0:T(8,128)S(1)}, f32[1,512,512]{2,1,0:T(8,128)S(1)},...) custom-call(s32[1]{0:T(128)S(6)} %copy.20.flag, bf16[128,8192]{1,0:T(8,128)(2,1)} %x_ref.1, ...), custom_call_target="tpu_custom_call" | custom-call | tf_op jit(solution)/shard_map/fused_step/pallas_call | solution.py:303
  67.9 1.0 %copy.21 = f32[1,512,512]{2,1,0:T(8,128)} copy(f32[1,512,512]{2,1,0:T(8,128)S(1)} %get-tuple-element.12) | data formatting | bytes 2097152
  68.9 1.0 %copy.22 = f32[1,512,512]{2,1,0:T(8,128)} copy(f32[1,512,512]{2,1,0:T(8,128)S(1)} %get-tuple-element.13) | data formatting | bytes 2097152
  69.9 1.0 %copy.23 = f32[1,512,512]{2,1,0:T(8,128)} copy(f32[1,512,512]{2,1,0:T(8,128)S(1)} %get-tuple-element.14) | data formatting | bytes 2097152
  70.8 1.0 %copy.24 = f32[1,512,512]{2,1,0:T(8,128)} copy(f32[1,512,512]{2,1,0:T(8,128)S(1)} %get-tuple-element.15) | data formatting | bytes 2097152
  71.8 1.0 %copy.25 = f32[1,512,512]{2,1,0:T(8,128)} copy(f32[1,512,512]{2,1,0:T(8,128)S(1)} %get-tuple-element.16) | data formatting | bytes 2097152
  72.8 0.7 copy.26
Async XLA Ops:
  1.3 0.9 %copy-start = (bf16[128,512]{1,0:T(8,128)(2,1)S(1)}, bf16[128,512]{1,0:T(8,128)(2,1)}, u32[]{:S(2)}) copy-start(bf16[128,512]{1,0:T(8,128)(2,1)} %g_ref.1) | copy-start | bytes 393220

commit v2 on v1

--- a/solution.py
+++ b/solution.py
@@ -29,20 +29,25 @@
     return dot(a_high, b_high) + (dot(a_high, b_low) + dot(a_low, b_high))
 
 
-def inverse_root(statistic):
-    shape = statistic.shape
+def inverse_roots(*statistics):
+    shape = statistics[0].shape
     eye = (lax.broadcasted_iota(jnp.int32, shape, 0) == lax.broadcasted_iota(jnp.int32, shape, 1)).astype(F32)
-    damped = statistic + DAMPING * eye
-    z = 2.5 / jnp.sqrt(jnp.sum(damped * damped, keepdims=True))
-    m = z * damped
-    p = dot(m, m)
-    r = 1.5625 * m - 0.625 * p + 0.0625 * dot(p, m)
-    w = 0.0625 * r + 0.1953125 * m - 0.01953125 * p
-    return jnp.sqrt(jnp.sqrt(z)) * (1.5625 * eye - 0.3125 * m - 0.48828125 * r + dot(w, r))
+    damped = [s + DAMPING * eye for s in statistics]
+    z = [2.5 / jnp.sqrt(jnp.sum(a * a, keepdims=True)) for a in damped]
+    m = [scale * a for scale, a in zip(z, damped)]
+    p = [dot(a, a) for a in m]
+    q = [dot(b, a) for a, b in zip(m, p)]
+    r = [1.5625 * a - 0.625 * b + 0.0625 * c for a, b, c in zip(m, p, q)]
+    w = [0.0625 * c + 0.1953125 * a - 0.01953125 * b for a, b, c in zip(m, p, r)]
+    last = [dot(a, b) for a, b in zip(w, r)]
+    return tuple(
+        jnp.sqrt(jnp.sqrt(scale)) * (1.5625 * eye - 0.3125 * a - 0.48828125 * b + c)
+        for scale, a, b, c in zip(z, m, r, last)
+    )
 
 
 def roots(left_stat, right_stat, left_old, right_old):
-    return (inverse_root(left_stat), inverse_root(right_stat))
+    return inverse_roots(left_stat, right_stat)
 
 
 def stale(left_stat, right_stat, left_old, right_old):
@@ -181,7 +186,8 @@
 
     steps = dict(g=g, h=h, i=i, y=y, x=x, p=p, d=d, s=s)
     for word in ORDER:
-        steps[word[0]](int(word[1:] or 0))
+        with jax.named_scope(word):
+            steps[word[0]](int(word[1:] or 0))
     return own_in[2], s_copy
 
 
@@ -201,12 +207,15 @@
 
     a_copy, b_copy = {}, {}
     ahead = near_part(row, 3)
-    for copy in arrived:
-        copy.wait()
-    for copy in u_copy:
-        copy.wait_recv()
-    for t in (3, 2, 1, 0):
-        a_out[t] = ((ahead if t == 3 else near_part(row, t)) + far_part(row, t)).astype(BF16)
+    with jax.named_scope("swap"):
+        for copy in arrived:
+            copy.wait()
+        for copy in u_copy:
+            copy.wait_recv()
+
+    def offer(t):
+        part = (ahead if t == 3 else near_part(row, t)) + far_part(row, t)
+        a_out[t] = part.astype(BF16)
         for k in range(2):
             a_copy[t, k] = go(a_out.at[t, halves[k]], a_in.at[t, halves[k]], a_s.at[2 * t + k], a_r.at[2 * t + k], (row, mine))
 
@@ -222,33 +231,42 @@
         b_out[t, halves[k]] = value.astype(BF16)
         b_copy[t, k] = go(b_out.at[t, halves[k]], b_in.at[t, halves[k]], b_s.at[2 * t + k], b_r.at[2 * t + k], (peer, mine))
 
-    total(3)
+    for t in (3, 2, 1, 0):
+        with jax.named_scope(f"offer{t}"):
+            offer(t)
+    with jax.named_scope("total3"):
+        total(3)
     for k in range(2):
-        pass_on(3, k, toggle(me, LINE))
-    total(2)
-    total(1)
-    total(0)
+        with jax.named_scope(f"pass3{k}"):
+            pass_on(3, k, toggle(me, LINE))
+    for t in (2, 1, 0):
+        with jax.named_scope(f"total{t}"):
+            total(t)
     for k in range(2):
-        pass_on(2, k, toggle(me, 2 * LINE), 3)
+        with jax.named_scope(f"pass2{k}"):
+            pass_on(2, k, toggle(me, 2 * LINE), 3)
     for k in range(2):
-        pass_on(1, k, toggle(me, LINE))
+        with jax.named_scope(f"pass1{k}"):
+            pass_on(1, k, toggle(me, LINE))
     for k in range(2):
-        a_copy[0, k].wait_recv()
-        value = tot[0, halves[k]] + a_in[0, halves[k]].astype(F32)
-        b_copy[2, k].wait_recv()
-        value = value + b_in[2, halves[k]].astype(F32)
-        b_copy[1, k].wait_recv()
-        q_ref[halves[k]] = (value + b_in[1, halves[k]].astype(F32)).astype(BF16)
+        with jax.named_scope(f"last{k}"):
+            a_copy[0, k].wait_recv()
+            value = tot[0, halves[k]] + a_in[0, halves[k]].astype(F32)
+            b_copy[2, k].wait_recv()
+            value = value + b_in[2, halves[k]].astype(F32)
+            b_copy[1, k].wait_recv()
+            q_ref[halves[k]] = (value + b_in[1, halves[k]].astype(F32)).astype(BF16)
 
 
 def step_kernel(n, rate, flag, x_ref, g_ref, w_hbm, ls_hbm, rs_hbm, lr_hbm, rr_hbm,
                 ls_out, rs_out, lr_out, rr_out, d_out, q_ref,
-                f, fs, ga, grad, w, ls, rs, lr, rr, d, u, us, tot, a_out, a_in, b_out, b_in,
+                f, fs, ga, grad, w, ls, rs, lr, rr, d, u, us, q, tot, a_out, a_in, b_out, b_in,
                 in_sem, out_sem, own, x_s, x_r, p_s, p_r, z_s, z_r, y_s, y_r, c_s, c_r, s_s, s_r, u_s, u_r, a_s, a_r, b_s, b_r):
     me, mine = lax.axis_index("dp"), lax.axis_index("owner")
     pair = flip(me, 1)
     block = w.shape[0]
-    greet([(toggle(me, k), mine) for k in range(1, n)] + [(me, 1 - mine)])
+    with jax.named_scope("greet"):
+        greet([(toggle(me, k), mine) for k in range(1, n)] + [(me, 1 - mine)])
     copies = Copies()
     ins = [
         pltpu.make_async_copy(src.at[0], dst, in_sem.at[k])
@@ -263,32 +281,45 @@
         pltpu.make_async_copy(src, dst.at[0], out_sem.at[k])
         for k, (src, dst) in enumerate(((ls, ls_out), (rs, rs_out), (lr, lr_out), (rr, rr_out), (d, d_out)))
     ]
-    grad[...] = grad[...] * (1.0 / (n * g_ref.shape[0]))
-    high = grad[...].astype(BF16)
-    for copy in ins:
-        copy.wait()
-    ls[...] = BETA * ls[...] + (1.0 - BETA) * dot(high, high, ((1,), (1,)))
-    outs[0].start()
-    rs[...] = BETA * rs[...] + (1.0 - BETA) * dot(high, high, ((0,), (0,)))
-    outs[1].start()
-    anew = jnp.full((block, block), flag[0], jnp.int32) > 0
-    lr[...] = jnp.where(anew, inverse_root(ls[...]), lr[...])
-    outs[2].start()
-    rr[...] = jnp.where(anew, inverse_root(rs[...]), rr[...])
-    outs[3].start()
-    direction = dot3(dot3(lr[...], grad[...]), rr[...])
-    norm = jnp.sqrt(jnp.sum(direction * direction, keepdims=True) + 1e-12)
-    direction = direction * (block / norm)
-    d[...] = direction
-    outs[4].start()
-    u[...] = (w[...] - rate * direction).astype(BF16)
-    u_copy = [copies.go(u, us, u_s.at[0], u_r.at[0], (pair, mine))]
+    with jax.named_scope("stats"):
+        for copy in ins:
+            copy.wait()
+        high = (grad[...] * (1.0 / (n * g_ref.shape[0]))).astype(BF16)
+        ls[...] = BETA * ls[...] + (1.0 - BETA) * dot(high, high, ((1,), (1,)))
+        rs[...] = BETA * rs[...] + (1.0 - BETA) * dot(high, high, ((0,), (0,)))
+        outs[0].start()
+        outs[1].start()
+    with jax.named_scope("roots"):
+        anew = jnp.full((block, block), flag[0], jnp.int32) > 0
+        left, right = inverse_roots(ls[...], rs[...])
+        lr[...] = jnp.where(anew, left, lr[...])
+        rr[...] = jnp.where(anew, right, rr[...])
+        outs[2].start()
+        outs[3].start()
+    with jax.named_scope("direction"):
+        d[...] = dot(dot(lr[...], high), rr[...])
+    with jax.named_scope("update"):
+        direction = d[...]
+        scale = block / jnp.sqrt(jnp.sum(direction * direction, keepdims=True) + 1e-12)
+    u_copy = []
+    for k in range(2):
+        with jax.named_scope(f"weights{k}"):
+            part = pl.ds(k * block // 2, block // 2)
+            u[part] = (w[part] - (rate * scale) * d[part]).astype(BF16)
+            u_copy.append(copies.go(u.at[part], us.at[part], u_s.at[k], u_r.at[k], (pair, mine)))
+    with jax.named_scope("scaled"):
+        d[...] = scale * d[...]
+        outs[4].start()
     for copy in s_copy.values():
         copy.wait_recv()
-    reduce_phase(n, copies, f, fs, u, us, [own_side], tot, a_out, a_in, b_out, b_in, a_s, a_r, b_s, b_r, u_copy, q_ref)
-    for copy in outs:
-        copy.wait()
-    copies.drain()
+    reduce_phase(n, copies, f, fs, u, us, [own_side], tot, a_out, a_in, b_out, b_in, a_s, a_r, b_s, b_r, u_copy, q)
+    with jax.named_scope("drain"):
+        q_out = pltpu.make_async_copy(q, q_ref, out_sem.at[5])
+        q_out.start()
+        q_out.wait()
+        for copy in outs:
+            copy.wait()
+        copies.drain()
 
 
 def fused_step(n, rate, inputs, out_grads, weights, left_stats, right_stats, left_roots, right_roots, refresh):
@@ -303,16 +334,38 @@
     return pl.pallas_call(
         functools.partial(step_kernel, n, rate),
         out_shape=[jax.ShapeDtypeStruct((1, block, block), F32)] * 5 + [jax.ShapeDtypeStruct((rows, width), BF16)],
-        in_specs=[pl.BlockSpec(memory_space=pltpu.SMEM)] + [anywhere] * 7,
-        out_specs=[anywhere] * 5 + [pl.BlockSpec(memory_space=pltpu.VMEM)],
+        in_specs=[pl.BlockSpec(memory_space=pltpu.SMEM)] + [pl.BlockSpec(memory_space=pltpu.HBM)] * 7,
+        out_specs=[anywhere] * 6,
         scratch_shapes=[
             pltpu.VMEM((n, rows, block), BF16), pltpu.VMEM((n // 2, rows, block), BF16), pltpu.VMEM((n, rows, width), BF16),
-        ] + [square] * 7 + [narrow] * 2 + [pltpu.VMEM((nz, rows, width), F32)] + [shards] * 4
-        + [dma((5,))] * 2 + [dma((3,))] + [dma((n,))] * 4 + [dma((LINE,))] * 4 + [dma((2 * LINE,))] * 2 + [dma((n,))] * 2
-        + [dma((1,))] * 2 + [dma((2 * LINE,))] * 4,
+        ] + [square] * 7 + [narrow] * 2 + [pltpu.VMEM((rows, width), BF16)] + [pltpu.VMEM((nz, rows, width), F32)] + [shards] * 4
+        + [dma((5,)), dma((6,)), dma((3,))] + [dma((n,))] * 4 + [dma((LINE,))] * 4 + [dma((2 * LINE,))] * 2 + [dma((n,))] * 2
+        + [dma((2,))] * 2 + [dma((2 * LINE,))] * 4,
         compiler_params=pltpu.CompilerParams(collective_id=0, has_side_effects=True, vmem_limit_bytes=48 << 20),
         name="fused_step",
-    )(refresh, inputs, out_grads, weights, left_stats, right_stats, left_roots, right_roots)
+    )(refresh, inputs, pltpu.with_memory_space_constraint(out_grads, pltpu.HBM), weights, left_stats, right_stats, left_roots, right_roots)
+
+
+def hand_out_kernel(*refs):
+    count = len(refs) // 2
+    copies = [pltpu.make_async_copy(refs[k], refs[count + k], refs[-1].at[k]) for k in range(count)]
+    for copy in copies:
+        copy.start()
+    for copy in copies:
+        copy.wait()
+
+
+def hand_out(*arrays):
+    anywhere = pl.BlockSpec(memory_space=pl.ANY)
+    return pl.pallas_call(
+        hand_out_kernel,
+        out_shape=[jax.ShapeDtypeStruct(a.shape, a.dtype) for a in arrays],
+        in_specs=[anywhere] * len(arrays),
+        out_specs=[pl.BlockSpec(memory_space=pltpu.HBM)] * len(arrays),
+        scratch_shapes=[pltpu.SemaphoreType.DMA((len(arrays),))],
+        compiler_params=pltpu.CompilerParams(vmem_limit_bytes=1 << 20),
+        name="hand_out",
+    )(*arrays)
 
 
 def body(inputs, out_grads, weights, left_stats, right_stats, left_roots, right_roots, refresh):
@@ -326,9 +379,9 @@
     kernels = col_blocks == 1 and lax.axis_size("owner") == 2 and replicas == 4 * LINE
     rate = 0.25 / math.sqrt(model_width)
     if kernels:
-        return fused_step(
+        return hand_out(*fused_step(
             replicas, rate, inputs, out_grads, weights, left_stats, right_stats, left_roots, right_roots, refresh
-        )
+        ))
     mine = lax.axis_index("dp") % col_blocks
     grads = lax.all_gather(out_grads, "dp", axis=0, tiled=True)
     grads = lax.dynamic_slice_in_dim(grads, mine * block, block, 1)

time: 73.6 us -> 67.7 us (0.920)
  local copies, waits for them, and re-layouts: 6.4 us -> 0 us
    unnamed x8 -> x0, local copies, waits for them, and re-layouts: 6.4 us -> none
    pallas_call x0 -> x1, Pallas kernels: none -> 2.41 us  [hand_out(): pl.pallas_call(hand_out_kernel, out_shape=[jax.ShapeDtypeStruct(a.shape,...]
    pallas_call x1, Pallas kernels: 65.7 us -> 63.9 us  [fused_step(): pl.pallas_call(functools.partial(step_kernel, n, rate), out_shape=[jax.Sh...]
where the time goes in v2:
time: 67.7 us; the launch traced here: 67.6 us
  Pallas kernels  66.3 us (98%)
  between operations  1.29 us (2%)
    pallas_call x1, Pallas kernels, fused_step(): pl.pallas_call(functools.partial(step_kernel, n, rate), out_shape=[jax.Sh...  63.9 us
    pallas_call x1, Pallas kernels, hand_out(): pl.pallas_call(hand_out_kernel, out_shape=[jax.ShapeDtypeStruct(a.shape,...  2.41 us

profile of v2, /device:TPU:0, one launch (start us, length us, event | category | flops | bytes accessed | tf_op | source)
XLA Modules:
  0.0 67.6 jit_solution(7447717022917676020)
XLA Ops:
  1.3 63.9 %fused_step.1 = (f32[1,512,512]{2,1,0:T(8,128)S(1)}, f32[1,512,512]{2,1,0:T(8,128)S(1)}, f32[1,512,512]{2,1,0:T(8,128)S(1)}, f32[1,512,512]{2,1,0:T(8,128)S(1)},...) custom-call(s32[1]{0:T(128)S(6)} %copy.14.flag, bf16[128,8192]{1,0:T(8,128)(2,1)} %x_ref.1, ...), custom_call_target="tpu_custom_call" | custom-call | tf_op jit(solution)/shard_map/fused_step/pallas_call | solution.py:334
  65.2 2.4 %hand_out.1 = (f32[1,512,512]{2,1,0:T(8,128)}, f32[1,512,512]{2,1,0:T(8,128)}, f32[1,512,512]{2,1,0:T(8,128)}, f32[1,512,512]{2,1,0:T(8,128)}, f32[1,512,512]{2,1,0:T(8,128)}, /*index=5*/bf16[128,512]{1,0:T(8,128)(2,1)}) custom-call(f32[1,512,512]{2,1,0:T(8,128)S(1)} %get-tuple-element.12.refs_0_, f32[1,512,512]{2,1,0:T(8,128)S(1)} %get-tuple-element.13.refs_1_, ...), custom_call_target="tpu_custom_call" | custom-call | tf_op jit(solution)/shard_map/hand_out/pallas_call | solution.py:360

commit v3 on v2

--- a/solution.py
+++ b/solution.py
@@ -91,28 +91,34 @@
 )
 
 
+PARTS = {9: 2, 13: 2}
+EXTRA = {(9, 1): 0, (13, 1): 16}
+
+
+def landed(view, sem):
+    pltpu.make_async_copy(view, view, sem).wait()
+
+
 class Copies:
-    def __init__(self):
-        self.sent = []
-
-    def go(self, src, dst, send, recv, peer):
-        copy = remote(src, dst, send, recv, peer)
-        copy.start()
-        self.sent.append(copy)
-        return copy
-
-    def drain(self):
-        for copy in self.sent:
-            copy.wait_send()
-
-
-def gather_phase(n, copies, x_ref, g_ref, f, fs, ga, grad, own, x_s, x_r, p_s, p_r, z_s, z_r, y_s, y_r, c_s, c_r, s_s, s_r):
+    def __init__(self, send):
+        self.send = send
+
+    def group(self, at):
+        def go(src, dst, recv, peer):
+            copy = remote(src, dst, self.send.at[at], recv, peer)
+            copy.start()
+            return copy
+
+        return go
+
+
+def gather_phase(n, copies, x_ref, g_ref, f, fs, ga, grad, own, x_r, p_r, z_r, y_r, c_r, s_r):
     me, mine = lax.axis_index("dp"), lax.axis_index("owner")
     rows, width = g_ref.shape
     half = rows // 2
-    near = pl.ds(pl.multiple_of(mine * half, half), half)
+    far = pl.ds(pl.multiple_of((1 - mine) * half, half), half)
     pair, row = flip(me, 1), flip(me, 2)
-    go = copies.go
+    go_x, go_g, go_s = copies.group(0), copies.group(1), copies.group(2)
 
     def cols(block):
         return pl.ds(pl.multiple_of(block * width, width), width)
@@ -122,24 +128,24 @@
         pltpu.make_async_copy(g_ref, ga.at[me], own.at[1]),
         pltpu.make_async_copy(x_ref.at[:, cols(pair)], fs.at[lax.div(me, 2)], own.at[2]),
     ]
-    x_copy, p_copy, z_copy, y_copy, c_copy, s_copy = {}, {}, {}, {}, {}, {}
+    x_copy, z_copy, y_copy, c_copy = {}, {}, {}, {}
 
     def fan(t, block):
         slot = toggle(me, LINE * t)
-        y_copy[t] = go(block, ga.at[slot], y_s.at[t], y_r.at[t], (row, mine))
-        c_copy[t] = go(block, ga.at[slot], c_s.at[t], c_r.at[t], (pair, mine))
+        y_copy[t] = go_g(block, ga.at[slot], y_r.at[t], (row, mine))
+        c_copy[t] = go_g(block, ga.at[slot], c_r.at[t], (pair, mine))
 
     def g(_):
         for copy in own_in:
             copy.start()
         for t in (2, 1):
-            z_copy[t] = go(g_ref, ga.at[me], z_s.at[t], z_r.at[t], (toggle(me, LINE * t), mine))
+            z_copy[t] = go_g(g_ref, ga.at[me], z_r.at[t], (toggle(me, LINE * t), mine))
         fan(0, g_ref)
 
     def h(_):
         z_copy[2].wait_recv()
         held = ga.at[toggle(me, LINE * 2)]
-        z_copy[3] = go(held, held, z_s.at[3], z_r.at[3], (toggle(me, LINE), mine))
+        z_copy[3] = go_g(held, held, z_r.at[3], (toggle(me, LINE), mine))
         fan(2, held)
 
     def i(t):
@@ -149,55 +155,67 @@
     def y(t):
         y_copy[t].wait_recv()
         held = ga.at[toggle(row, LINE * t)]
-        c_copy[LINE + t] = go(held, held, c_s.at[LINE + t], c_r.at[LINE + t], (pair, mine))
+        c_copy[LINE + t] = go_g(held, held, c_r.at[LINE + t], (pair, mine))
+
+    def slices(k):
+        count = PARTS.get(k, 1)
+        span = half // count
+        return [pl.ds(pl.multiple_of(mine * half + at * span, span), span) for at in range(count)]
 
     def x(k):
         peer = toggle(me, k)
         if k == 1:
-            src, dst = x_ref.at[:, cols(peer)], f.at[me]
+            x_copy[k] = [go_x(x_ref.at[:, cols(peer)], f.at[me], x_r.at[k], (peer, mine))]
+            return
+        x_copy[k] = []
+        for at, part in enumerate(slices(k)):
+            sem = x_r.at[k if at == 0 else EXTRA[k, at]]
+            x_copy[k].append(go_x(x_ref.at[part, cols(peer)], f.at[me, part], sem, (peer, mine)))
+
+    def p(k):
+        if k == 1:
+            x_copy[k][0].wait_recv()
+            return
+        for at, part in enumerate(slices(k)):
+            x_copy[k][at].wait_recv()
+            held = f.at[toggle(me, k), part]
+            go_x(held, held, p_r.at[k // 2], (me, 1 - mine))
+
+    def d(k):
+        chip = pl.ds(pl.multiple_of(2 * lax.div(toggle(me, k), 2), 2), 2)
+        if k:
+            landed(f.at[chip, far], p_r.at[k // 2])
         else:
-            src, dst = x_ref.at[near, cols(peer)], f.at[me, near]
-        x_copy[k] = go(src, dst, x_s.at[k], x_r.at[k], (peer, mine))
-
-    def p(k):
-        x_copy[k].wait_recv()
-        if k > 1:
-            held = f.at[toggle(me, k), near]
-            p_copy[k] = go(held, held, p_s.at[k], p_r.at[k], (me, 1 - mine))
-
-    def d(k):
-        for at in (k, k + 1):
-            if at > 1:
-                p_copy[at].wait_recv()
-        if k == 0:
             own_in[0].wait()
             own_in[1].wait()
         t = k // LINE
         c_copy[t + LINE if k % LINE else t].wait_recv()
-        chip = pl.multiple_of(2 * lax.div(toggle(me, k), 2), 2)
-        term = dot(
-            f[pl.ds(chip, 2)].reshape(2 * rows, width), ga[pl.ds(chip, 2)].reshape(2 * rows, width), ((0,), (0,))
-        )
+        term = dot(f[chip].reshape(2 * rows, width), ga[chip].reshape(2 * rows, width), ((0,), (0,)))
         grad[...] = term if k == 0 else grad[...] + term
 
     def s(k):
         source = toggle(me, k)
-        s_copy[k] = go(f.at[source], fs.at[lax.div(source, 2)], s_s.at[k], s_r.at[k], (pair, mine))
+        go_s(f.at[source], fs.at[lax.div(source, 2)], s_r.at[0], (pair, mine))
 
     steps = dict(g=g, h=h, i=i, y=y, x=x, p=p, d=d, s=s)
     for word in ORDER:
         with jax.named_scope(word):
             steps[word[0]](int(word[1:] or 0))
-    return own_in[2], s_copy
-
-
-def reduce_phase(n, copies, f, fs, u, us, arrived, tot, a_out, a_in, b_out, b_in, a_s, a_r, b_s, b_r, u_copy, q_ref):
+    return own_in[2]
+
+
+def reduce_phase(copies, f, fs, u, us, arrive, q, tot, keep, a_out, a_in, b_out, b_in, e_out, e_in, h_out, h_in, g_out, g_in,
+                 a_r, b_r, e_r):
     me, mine = lax.axis_index("dp"), lax.axis_index("owner")
     row = flip(me, 2)
-    rows = q_ref.shape[0]
-    half = rows // 2
-    go = copies.go
-    halves = [pl.ds(k * half, half) for k in range(2)]
+    rows = q.shape[0]
+    cut = rows // 4
+    half = (rows - cut) // 2
+    go = copies.group(3)
+    first = pl.ds(0, cut)
+    rest = [pl.ds(cut + k * half, half) for k in range(2)]
+    spans = [pl.ds(k * half, half) for k in range(2)]
+    near_z, far_z, across = (toggle(me, LINE), mine), (toggle(me, 2 * LINE), mine), (row, mine)
 
     def near_part(base, t):
         return dot(f[toggle(base, LINE * t)], u[...])
@@ -208,75 +226,118 @@
     a_copy, b_copy = {}, {}
     ahead = near_part(row, 3)
     with jax.named_scope("swap"):
-        for copy in arrived:
-            copy.wait()
-        for copy in u_copy:
-            copy.wait_recv()
-
-    def offer(t):
-        part = (ahead if t == 3 else near_part(row, t)) + far_part(row, t)
-        a_out[t] = part.astype(BF16)
-        for k in range(2):
-            a_copy[t, k] = go(a_out.at[t, halves[k]], a_in.at[t, halves[k]], a_s.at[2 * t + k], a_r.at[2 * t + k], (row, mine))
-
-    def total(t):
-        tot[t] = near_part(me, t) + far_part(me, t)
+        arrive()
+
+    def part(base, t):
+        return near_part(base, t) + far_part(base, t)
+
+    def early(k, value):
+        e_out[k] = value[:cut].astype(BF16)
+        go(e_out.at[k], e_in.at[k], e_r.at[k // 2], near_z)
+
+    def stage(t, value):
+        a_out[t] = value[cut:].astype(BF16)
+
+    def offer(t, k):
+        a_copy[t, k] = go(a_out.at[t, spans[k]], a_in.at[t, spans[k]], a_r.at[2 * t + k], across)
 
     def pass_on(t, k, peer, extra=None):
         a_copy[t, k].wait_recv()
-        value = tot[t, halves[k]] + a_in[t, halves[k]].astype(F32)
+        value = tot[t, rest[k]] + a_in[t, spans[k]].astype(F32)
         if extra is not None:
             b_copy[extra, k].wait_recv()
-            value = value + b_in[extra, halves[k]].astype(F32)
-        b_out[t, halves[k]] = value.astype(BF16)
-        b_copy[t, k] = go(b_out.at[t, halves[k]], b_in.at[t, halves[k]], b_s.at[2 * t + k], b_r.at[2 * t + k], (peer, mine))
-
-    for t in (3, 2, 1, 0):
-        with jax.named_scope(f"offer{t}"):
-            offer(t)
+            value = value + b_in[extra, spans[k]].astype(F32)
+        b_out[t, spans[k]] = value.astype(BF16)
+        b_copy[t, k] = go(b_out.at[t, spans[k]], b_in.at[t, spans[k]], b_r.at[2 * t + k], peer)
+
+    with jax.named_scope("offer3"):
+        value = ahead + far_part(row, 3)
+        stage(3, value)
+        offer(3, 0)
+        offer(3, 1)
+        early(0, value)
+    with jax.named_scope("offer1"):
+        value = part(row, 1)
+        early(1, value)
+        stage(1, value)
     with jax.named_scope("total3"):
-        total(3)
-    for k in range(2):
-        with jax.named_scope(f"pass3{k}"):
-            pass_on(3, k, toggle(me, LINE))
-    for t in (2, 1, 0):
-        with jax.named_scope(f"total{t}"):
-            total(t)
+        value = part(me, 3)
+        early(2, value)
+        tot[3] = value
+    with jax.named_scope("offer2"):
+        value = part(row, 2)
+        stage(2, value)
+        offer(2, 0)
+        offer(2, 1)
+        keep[0] = value[:cut]
+    with jax.named_scope("total1"):
+        value = part(me, 1)
+        early(3, value)
+        tot[1] = value
+    with jax.named_scope("offer0"):
+        value = part(row, 0)
+        stage(0, value)
+        keep[1] = value[:cut]
+    with jax.named_scope("pass30"):
+        pass_on(3, 0, near_z)
+    with jax.named_scope("total2"):
+        tot[2] = part(me, 2)
+    with jax.named_scope("pass31"):
+        pass_on(3, 1, near_z)
+    with jax.named_scope("hop"):
+        landed(e_in.at[pl.ds(0, 2)], e_r.at[0])
+        h_copy = []
+        for k in range(2):
+            h_out[k] = (keep[k] + e_in[k].astype(F32)).astype(BF16)
+            h_copy.append(go(h_out.at[k], h_in.at[k], e_r.at[3 + k], across))
+    for t in (1, 0):
+        offer(t, 0)
+        offer(t, 1)
+    with jax.named_scope("total0"):
+        tot[0] = part(me, 0)
     for k in range(2):
         with jax.named_scope(f"pass2{k}"):
-            pass_on(2, k, toggle(me, 2 * LINE), 3)
-    for k in range(2):
-        with jax.named_scope(f"pass1{k}"):
-            pass_on(1, k, toggle(me, LINE))
+            pass_on(2, k, far_z, 3)
+    with jax.named_scope("hand"):
+        landed(e_in.at[pl.ds(2, 2)], e_r.at[1])
+        h_copy[0].wait_recv()
+        g_out[...] = (tot[2, first] + e_in[2].astype(F32) + h_in[0].astype(F32)).astype(BF16)
+        g_copy = go(g_out, g_in, e_r.at[2], far_z)
+    with jax.named_scope("pass10"):
+        pass_on(1, 0, near_z)
+    with jax.named_scope("pass11"):
+        pass_on(1, 1, near_z)
+    with jax.named_scope("first"):
+        h_copy[1].wait_recv()
+        g_copy.wait_recv()
+        q[first] = (tot[0, first] + e_in[3].astype(F32) + h_in[1].astype(F32) + g_in[...].astype(F32)).astype(BF16)
     for k in range(2):
         with jax.named_scope(f"last{k}"):
             a_copy[0, k].wait_recv()
-            value = tot[0, halves[k]] + a_in[0, halves[k]].astype(F32)
-            b_copy[2, k].wait_recv()
-            value = value + b_in[2, halves[k]].astype(F32)
-            b_copy[1, k].wait_recv()
-            q_ref[halves[k]] = (value + b_in[1, halves[k]].astype(F32)).astype(BF16)
+            value = tot[0, rest[k]] + a_in[0, spans[k]].astype(F32)
+            for t in (2, 1):
+                b_copy[t, k].wait_recv()
+                value = value + b_in[t, spans[k]].astype(F32)
+            q[rest[k]] = value.astype(BF16)
 
 
 def step_kernel(n, rate, flag, x_ref, g_ref, w_hbm, ls_hbm, rs_hbm, lr_hbm, rr_hbm,
                 ls_out, rs_out, lr_out, rr_out, d_out, q_ref,
-                f, fs, ga, grad, w, ls, rs, lr, rr, d, u, us, q, tot, a_out, a_in, b_out, b_in,
-                in_sem, out_sem, own, x_s, x_r, p_s, p_r, z_s, z_r, y_s, y_r, c_s, c_r, s_s, s_r, u_s, u_r, a_s, a_r, b_s, b_r):
+                f, fs, ga, grad, w, ls, rs, lr, rr, d, u, us, q, tot, keep, a_out, a_in, b_out, b_in, e_out, e_in, h_out, h_in, g_out, g_in,
+                in_sem, out_sem, send, own, x_r, p_r, z_r, y_r, c_r, s_r, u_r, a_r, b_r, e_r):
     me, mine = lax.axis_index("dp"), lax.axis_index("owner")
     pair = flip(me, 1)
     block = w.shape[0]
     with jax.named_scope("greet"):
         greet([(toggle(me, k), mine) for k in range(1, n)] + [(me, 1 - mine)])
-    copies = Copies()
+    copies = Copies(send)
     ins = [
         pltpu.make_async_copy(src.at[0], dst, in_sem.at[k])
         for k, (src, dst) in enumerate(((ls_hbm, ls), (rs_hbm, rs), (lr_hbm, lr), (rr_hbm, rr), (w_hbm, w)))
     ]
     for copy in ins:
         copy.start()
-    own_side, s_copy = gather_phase(
-        n, copies, x_ref, g_ref, f, fs, ga, grad, own, x_s, x_r, p_s, p_r, z_s, z_r, y_s, y_r, c_s, c_r, s_s, s_r
-    )
+    own_side = gather_phase(n, copies, x_ref, g_ref, f, fs, ga, grad, own, x_r, p_r, z_r, y_r, c_r, s_r)
     outs = [
         pltpu.make_async_copy(src, dst.at[0], out_sem.at[k])
         for k, (src, dst) in enumerate(((ls, ls_out), (rs, rs_out), (lr, lr_out), (rr, rr_out), (d, d_out)))
@@ -301,25 +362,32 @@
     with jax.named_scope("update"):
         direction = d[...]
         scale = block / jnp.sqrt(jnp.sum(direction * direction, keepdims=True) + 1e-12)
-    u_copy = []
     for k in range(2):
         with jax.named_scope(f"weights{k}"):
             part = pl.ds(k * block // 2, block // 2)
             u[part] = (w[part] - (rate * scale) * d[part]).astype(BF16)
-            u_copy.append(copies.go(u.at[part], us.at[part], u_s.at[k], u_r.at[k], (pair, mine)))
+            copies.group(2)(u.at[part], us.at[part], u_r.at[0], (pair, mine))
     with jax.named_scope("scaled"):
         d[...] = scale * d[...]
         outs[4].start()
-    for copy in s_copy.values():
-        copy.wait_recv()
-    reduce_phase(n, copies, f, fs, u, us, [own_side], tot, a_out, a_in, b_out, b_in, a_s, a_r, b_s, b_r, u_copy, q)
+
+    def arrive():
+        own_side.wait()
+        landed(fs.at[pl.ds(0, n // 2 - 1)], s_r.at[0])
+        landed(us, u_r.at[0])
+
+    reduce_phase(
+        copies, f, fs, u, us, arrive, q, tot, keep,
+        a_out, a_in, b_out, b_in, e_out, e_in, h_out, h_in, g_out, g_in, a_r, b_r, e_r,
+    )
     with jax.named_scope("drain"):
         q_out = pltpu.make_async_copy(q, q_ref, out_sem.at[5])
         q_out.start()
         q_out.wait()
         for copy in outs:
             copy.wait()
-        copies.drain()
+        for at, units in enumerate((n - 1, n - 1, n // 2 + 3, n // 2 - 1)):
+            landed(f.at[pl.ds(0, units)], send.at[at])
 
 
 def fused_step(n, rate, inputs, out_grads, weights, left_stats, right_stats, left_roots, right_roots, refresh):
@@ -330,7 +398,8 @@
     anywhere = pl.BlockSpec(memory_space=pl.ANY)
     square = pltpu.VMEM((block, block), F32)
     narrow = pltpu.VMEM((block, block), BF16)
-    shards = pltpu.VMEM((nz, rows, width), BF16)
+    cut = rows // 4
+    shards = pltpu.VMEM((nz, rows - cut, width), BF16)
     return pl.pallas_call(
         functools.partial(step_kernel, n, rate),
         out_shape=[jax.ShapeDtypeStruct((1, block, block), F32)] * 5 + [jax.ShapeDtypeStruct((rows, width), BF16)],
@@ -338,9 +407,11 @@
         out_specs=[anywhere] * 6,
         scratch_shapes=[
             pltpu.VMEM((n, rows, block), BF16), pltpu.VMEM((n // 2, rows, block), BF16), pltpu.VMEM((n, rows, width), BF16),
-        ] + [square] * 7 + [narrow] * 2 + [pltpu.VMEM((rows, width), BF16)] + [pltpu.VMEM((nz, rows, width), F32)] + [shards] * 4
-        + [dma((5,)), dma((6,)), dma((3,))] + [dma((n,))] * 4 + [dma((LINE,))] * 4 + [dma((2 * LINE,))] * 2 + [dma((n,))] * 2
-        + [dma((2,))] * 2 + [dma((2 * LINE,))] * 4,
+        ] + [square] * 7 + [narrow] * 2 + [pltpu.VMEM((rows, width), BF16)] + [pltpu.VMEM((nz, rows, width), F32), pltpu.VMEM((2, cut, width), F32)] + [shards] * 4
+        + [pltpu.VMEM((4, cut, width), BF16)] * 2 + [pltpu.VMEM((2, cut, width), BF16)] * 2 + [pltpu.VMEM((cut, width), BF16)] * 2
+        + [dma((5,)), dma((6,)), dma((4,)), dma((3,))]
+        + [dma((n + len(EXTRA) - 1,)), dma((n // 2,)), dma((LINE,)), dma((LINE,)), dma((2 * LINE,)), dma((1,)), dma((1,))]
+        + [dma((2 * LINE,)), dma((2 * LINE,)), dma((5,))],
         compiler_params=pltpu.CompilerParams(collective_id=0, has_side_effects=True, vmem_limit_bytes=48 << 20),
         name="fused_step",
     )(refresh, inputs, pltpu.with_memory_space_constraint(out_grads, pltpu.HBM), weights, left_stats, right_stats, left_roots, right_roots)
@@ -376,7 +447,7 @@
     col_blocks = col_count // block
     replicas = lax.axis_size("dp")
     tok_total = tok_local * replicas
-    kernels = col_blocks == 1 and lax.axis_size("owner") == 2 and replicas == 4 * LINE
+    kernels = col_blocks == 1 and lax.axis_size("owner") == 2 and replicas == 4 * LINE and block == 4 * tok_local
     rate = 0.25 / math.sqrt(model_width)
     if kernels:
         return hand_out(*fused_step(

time: 67.7 us -> 66 us (0.975)
  Pallas kernels: 66.3 us -> 64.6 us
    pallas_call x1, Pallas kernels: 63.9 us -> 62.2 us  [fused_step(): pl.pallas_call(functools.partial(step_kernel, n, rate), out_shape=[jax.Sh...]
where the time goes in v3:
time: 66 us; the launch traced here: 65.9 us
  Pallas kernels  64.6 us (98%)
  between operations  1.29 us (2%)
    pallas_call x1, Pallas kernels, fused_step(): pl.pallas_call(functools.partial(step_kernel, n, rate), out_shape=[jax.Sh...  62.2 us
    pallas_call x1, Pallas kernels, hand_out(): pl.pallas_call(hand_out_kernel, out_shape=[jax.ShapeDtypeStruct(a.shape,...  2.41 us

profile of v3, /device:TPU:0, one launch (start us, length us, event | category | flops | bytes accessed | tf_op | source)
XLA Modules:
  0.0 65.9 jit_solution(12125443975376957867)
XLA Ops:
  1.3 62.2 %fused_step.1 = (f32[1,512,512]{2,1,0:T(8,128)S(1)}, f32[1,512,512]{2,1,0:T(8,128)S(1)}, f32[1,512,512]{2,1,0:T(8,128)S(1)}, f32[1,512,512]{2,1,0:T(8,128)S(1)},...) custom-call(s32[1]{0:T(128)S(6)} %copy.14.flag, bf16[128,8192]{1,0:T(8,128)(2,1)} %x_ref.1, ...), custom_call_target="tpu_custom_call" | custom-call | tf_op jit(solution)/shard_map/fused_step/pallas_call | solution.py:403
  63.5 2.4 %hand_out.1 = (f32[1,512,512]{2,1,0:T(8,128)}, f32[1,512,512]{2,1,0:T(8,128)}, f32[1,512,512]{2,1,0:T(8,128)}, f32[1,512,512]{2,1,0:T(8,128)}, f32[1,512,512]{2,1,0:T(8,128)}, /*index=5*/bf16[128,512]{1,0:T(8,128)(2,1)}) custom-call(f32[1,512,512]{2,1,0:T(8,128)S(1)} %get-tuple-element.12.refs_0_, f32[1,512,512]{2,1,0:T(8,128)S(1)} %get-tuple-element.13.refs_1_, ...), custom_call_target="tpu_custom_call" | custom-call | tf_op jit(solution)/shard_map/hand_out/pallas_call | solution.py:431

commit v4 on v3

--- a/solution.py
+++ b/solution.py
@@ -29,17 +29,31 @@
     return dot(a_high, b_high) + (dot(a_high, b_low) + dot(a_low, b_high))
 
 
+def even_dot(a, b, dims=((1,), (0,))):
+    half = a.shape[0] // 2
+    a, b = a.astype(BF16), b.astype(BF16)
+
+    def cut(x, axis, low):
+        return (x[:half] if low else x[half:]) if axis == 0 else (x[:, :half] if low else x[:, half:])
+
+    over, under = (cut(a, 1 - dims[0][0], low) for low in (True, False))
+    upper = dot(over, b, dims)
+    corner = dot(under, cut(b, 1 - dims[1][0], False), dims)
+    return jnp.concatenate([upper, jnp.concatenate([upper[:, half:].T, corner], axis=1)], axis=0)
+
+
 def inverse_roots(*statistics):
     shape = statistics[0].shape
     eye = (lax.broadcasted_iota(jnp.int32, shape, 0) == lax.broadcasted_iota(jnp.int32, shape, 1)).astype(F32)
     damped = [s + DAMPING * eye for s in statistics]
+    squares = [even_dot(a, a) for a in damped]
     z = [2.5 / jnp.sqrt(jnp.sum(a * a, keepdims=True)) for a in damped]
     m = [scale * a for scale, a in zip(z, damped)]
-    p = [dot(a, a) for a in m]
-    q = [dot(b, a) for a, b in zip(m, p)]
+    p = [(scale * scale) * a for scale, a in zip(z, squares)]
+    q = [even_dot(b, a) for a, b in zip(m, p)]
     r = [1.5625 * a - 0.625 * b + 0.0625 * c for a, b, c in zip(m, p, q)]
     w = [0.0625 * c + 0.1953125 * a - 0.01953125 * b for a, b, c in zip(m, p, r)]
-    last = [dot(a, b) for a, b in zip(w, r)]
+    last = [even_dot(a, b) for a, b in zip(w, r)]
     return tuple(
         jnp.sqrt(jnp.sqrt(scale)) * (1.5625 * eye - 0.3125 * a - 0.48828125 * b + c)
         for scale, a, b, c in zip(z, m, r, last)
@@ -279,7 +293,7 @@
         stage(0, value)
         keep[1] = value[:cut]
     with jax.named_scope("pass30"):
-        pass_on(3, 0, near_z)
+        pass_on(3, 0, (toggle(me, 3 * LINE), mine))
     with jax.named_scope("total2"):
         tot[2] = part(me, 2)
     with jax.named_scope("pass31"):
@@ -297,7 +311,7 @@
         tot[0] = part(me, 0)
     for k in range(2):
         with jax.named_scope(f"pass2{k}"):
-            pass_on(2, k, far_z, 3)
+            pass_on(2, k, far_z, 3 if k else None)
     with jax.named_scope("hand"):
         landed(e_in.at[pl.ds(2, 2)], e_r.at[1])
         h_copy[0].wait_recv()
@@ -315,7 +329,7 @@
         with jax.named_scope(f"last{k}"):
             a_copy[0, k].wait_recv()
             value = tot[0, rest[k]] + a_in[0, spans[k]].astype(F32)
-            for t in (2, 1):
+            for t in (2, 1) if k else (3, 2, 1):
                 b_copy[t, k].wait_recv()
                 value = value + b_in[t, spans[k]].astype(F32)
             q[rest[k]] = value.astype(BF16)
@@ -346,8 +360,8 @@
         for copy in ins:
             copy.wait()
         high = (grad[...] * (1.0 / (n * g_ref.shape[0]))).astype(BF16)
-        ls[...] = BETA * ls[...] + (1.0 - BETA) * dot(high, high, ((1,), (1,)))
-        rs[...] = BETA * rs[...] + (1.0 - BETA) * dot(high, high, ((0,), (0,)))
+        ls[...] = BETA * ls[...] + (1.0 - BETA) * even_dot(high, high, ((1,), (1,)))
+        rs[...] = BETA * rs[...] + (1.0 - BETA) * even_dot(high, high, ((0,), (0,)))
         outs[0].start()
         outs[1].start()
     with jax.named_scope("roots"):
@@ -358,10 +372,16 @@
         outs[2].start()
         outs[3].start()
     with jax.named_scope("direction"):
-        d[...] = dot(dot(lr[...], high), rr[...])
+        through = dot(lr[...], high).astype(BF16)
+        last = rr[...].astype(BF16)
+        total = jnp.zeros((8, block), F32)
+        for k in range(4):
+            span = block // 4
+            value = dot(through[k * span : (k + 1) * span], last)
+            d[pl.ds(k * span, span)] = value
+            total = total + jnp.sum((value * value).reshape(span // 8, 8, block), axis=0)
     with jax.named_scope("update"):
-        direction = d[...]
-        scale = block / jnp.sqrt(jnp.sum(direction * direction, keepdims=True) + 1e-12)
+        scale = block / jnp.sqrt(jnp.sum(total, keepdims=True) + 1e-12)
     for k in range(2):
         with jax.named_scope(f"weights{k}"):
             part = pl.ds(k * block // 2, block // 2)

time: 66 us -> 64.7 us (0.980)
  Pallas kernels: 64.6 us -> 63.3 us
    pallas_call x1, Pallas kernels: 62.2 us -> 60.9 us  [fused_step(): pl.pallas_call(functools.partial(step_kernel, n, rate), out_shape=[jax.Sh...]
where the time goes in v4:
time: 64.7 us; the launch traced here: 64.6 us
  Pallas kernels  63.3 us (98%)
  between operations  1.29 us (2%)
    pallas_call x1, Pallas kernels, fused_step(): pl.pallas_call(functools.partial(step_kernel, n, rate), out_shape=[jax.Sh...  60.9 us
    pallas_call x1, Pallas kernels, hand_out(): pl.pallas_call(hand_out_kernel, out_shape=[jax.ShapeDtypeStruct(a.shape,...  2.41 us

profile of v4, /device:TPU:0, one launch (start us, length us, event | category | flops | bytes accessed | tf_op | source)
XLA Modules:
  0.0 64.6 jit_solution(7728078694343901632)
XLA Ops:
  1.3 60.9 %fused_step.1 = (f32[1,512,512]{2,1,0:T(8,128)S(1)}, f32[1,512,512]{2,1,0:T(8,128)S(1)}, f32[1,512,512]{2,1,0:T(8,128)S(1)}, f32[1,512,512]{2,1,0:T(8,128)S(1)},...) custom-call(s32[1]{0:T(128)S(6)} %copy.14.flag, bf16[128,8192]{1,0:T(8,128)(2,1)} %x_ref.1, ...), custom_call_target="tpu_custom_call" | custom-call | tf_op jit(solution)/shard_map/fused_step/pallas_call | solution.py:423
  62.1 2.4 %hand_out.1 = (f32[1,512,512]{2,1,0:T(8,128)}, f32[1,512,512]{2,1,0:T(8,128)}, f32[1,512,512]{2,1,0:T(8,128)}, f32[1,512,512]{2,1,0:T(8,128)}, f32[1,512,512]{2,1,0:T(8,128)}, /*index=5*/bf16[128,512]{1,0:T(8,128)(2,1)}) custom-call(f32[1,512,512]{2,1,0:T(8,128)S(1)} %get-tuple-element.12.refs_0_, f32[1,512,512]{2,1,0:T(8,128)S(1)} %get-tuple-element.13.refs_1_, ...), custom_call_target="tpu_custom_call" | custom-call | tf_op jit(solution)/shard_map/hand_out/pallas_call | solution.py:451

commit v5 on v4

--- a/solution.py
+++ b/solution.py
@@ -113,6 +113,16 @@
     pltpu.make_async_copy(view, view, sem).wait()
 
 
+HIGH = (
+    "o3", "s3", "o1", "t3", "o2", "s2", "t1", "o0", "p30", "t2", "p31", "h", "s1", "s0", "t0",
+    "p20", "p21", "g", "p10", "p11", "f", "q0", "q1",
+)
+LOW = (
+    "o1", "s1", "o3", "s3", "t1", "o2", "t3", "o0", "p10", "t2", "p11", "h", "s2", "s0", "t0",
+    "p30", "p31", "g", "p20", "p21", "f", "q0", "q1",
+)
+
+
 class Copies:
     def __init__(self, send):
         self.send = send
@@ -218,7 +228,7 @@
     return own_in[2]
 
 
-def reduce_phase(copies, f, fs, u, us, arrive, q, tot, keep, a_out, a_in, b_out, b_in, e_out, e_in, h_out, h_in, g_out, g_in,
+def reduce_phase(order, copies, feats, fs, u, us, arrive, q, tot, keep, a_out, a_in, b_out, b_in, e_out, e_in, h_out, h_in, g_out, g_in,
                  a_r, b_r, e_r):
     me, mine = lax.axis_index("dp"), lax.axis_index("owner")
     row = flip(me, 2)
@@ -229,110 +239,85 @@
     first = pl.ds(0, cut)
     rest = [pl.ds(cut + k * half, half) for k in range(2)]
     spans = [pl.ds(k * half, half) for k in range(2)]
-    near_z, far_z, across = (toggle(me, LINE), mine), (toggle(me, 2 * LINE), mine), (row, mine)
+    near_z, far_z, direct, across = (toggle(me, LINE), mine), (toggle(me, 2 * LINE), mine), (toggle(me, 3 * LINE), mine), (row, mine)
 
     def near_part(base, t):
-        return dot(f[toggle(base, LINE * t)], u[...])
+        return dot(feats[toggle(base, LINE * t)], u[...])
 
     def far_part(base, t):
         return dot(fs[lax.div(toggle(base, LINE * t), 2)], us[...])
 
-    a_copy, b_copy = {}, {}
-    ahead = near_part(row, 3)
+    a_copy, b_copy, h_copy, g_copy = {}, {}, [], []
+    lead = int(order[0][1])
+    ahead = near_part(row, lead)
     with jax.named_scope("swap"):
         arrive()
 
-    def part(base, t):
-        return near_part(base, t) + far_part(base, t)
+    def o(t):
+        value = (ahead if t == lead else near_part(row, t)) + far_part(row, t)
+        a_out[t] = value[cut:].astype(BF16)
+        if t % 2:
+            early(0 if t == 3 else 1, value)
+        else:
+            keep[0 if t == 2 else 1] = value[:cut]
+
+    def t(t):
+        value = near_part(me, t) + far_part(me, t)
+        if t % 2:
+            early(2 if t == 3 else 3, value)
+        tot[t] = value
 
     def early(k, value):
         e_out[k] = value[:cut].astype(BF16)
         go(e_out.at[k], e_in.at[k], e_r.at[k // 2], near_z)
 
-    def stage(t, value):
-        a_out[t] = value[cut:].astype(BF16)
-
-    def offer(t, k):
-        a_copy[t, k] = go(a_out.at[t, spans[k]], a_in.at[t, spans[k]], a_r.at[2 * t + k], across)
-
-    def pass_on(t, k, peer, extra=None):
+    def s(t):
+        for k in range(2):
+            a_copy[t, k] = go(a_out.at[t, spans[k]], a_in.at[t, spans[k]], a_r.at[2 * t + k], across)
+
+    def p(t, k):
         a_copy[t, k].wait_recv()
         value = tot[t, rest[k]] + a_in[t, spans[k]].astype(F32)
-        if extra is not None:
-            b_copy[extra, k].wait_recv()
-            value = value + b_in[extra, spans[k]].astype(F32)
+        peer = near_z
+        if t == 2:
+            peer = far_z
+            if k:
+                b_copy[3, k].wait_recv()
+                value = value + b_in[3, spans[k]].astype(F32)
+        elif (t, k) == (3, 0):
+            peer = direct
         b_out[t, spans[k]] = value.astype(BF16)
         b_copy[t, k] = go(b_out.at[t, spans[k]], b_in.at[t, spans[k]], b_r.at[2 * t + k], peer)
 
-    with jax.named_scope("offer3"):
-        value = ahead + far_part(row, 3)
-        stage(3, value)
-        offer(3, 0)
-        offer(3, 1)
-        early(0, value)
-    with jax.named_scope("offer1"):
-        value = part(row, 1)
-        early(1, value)
-        stage(1, value)
-    with jax.named_scope("total3"):
-        value = part(me, 3)
-        early(2, value)
-        tot[3] = value
-    with jax.named_scope("offer2"):
-        value = part(row, 2)
-        stage(2, value)
-        offer(2, 0)
-        offer(2, 1)
-        keep[0] = value[:cut]
-    with jax.named_scope("total1"):
-        value = part(me, 1)
-        early(3, value)
-        tot[1] = value
-    with jax.named_scope("offer0"):
-        value = part(row, 0)
-        stage(0, value)
-        keep[1] = value[:cut]
-    with jax.named_scope("pass30"):
-        pass_on(3, 0, (toggle(me, 3 * LINE), mine))
-    with jax.named_scope("total2"):
-        tot[2] = part(me, 2)
-    with jax.named_scope("pass31"):
-        pass_on(3, 1, near_z)
-    with jax.named_scope("hop"):
+    def h():
         landed(e_in.at[pl.ds(0, 2)], e_r.at[0])
-        h_copy = []
         for k in range(2):
             h_out[k] = (keep[k] + e_in[k].astype(F32)).astype(BF16)
             h_copy.append(go(h_out.at[k], h_in.at[k], e_r.at[3 + k], across))
-    for t in (1, 0):
-        offer(t, 0)
-        offer(t, 1)
-    with jax.named_scope("total0"):
-        tot[0] = part(me, 0)
-    for k in range(2):
-        with jax.named_scope(f"pass2{k}"):
-            pass_on(2, k, far_z, 3 if k else None)
-    with jax.named_scope("hand"):
+
+    def g():
         landed(e_in.at[pl.ds(2, 2)], e_r.at[1])
         h_copy[0].wait_recv()
         g_out[...] = (tot[2, first] + e_in[2].astype(F32) + h_in[0].astype(F32)).astype(BF16)
-        g_copy = go(g_out, g_in, e_r.at[2], far_z)
-    with jax.named_scope("pass10"):
-        pass_on(1, 0, near_z)
-    with jax.named_scope("pass11"):
-        pass_on(1, 1, near_z)
-    with jax.named_scope("first"):
+        g_copy.append(go(g_out, g_in, e_r.at[2], far_z))
+
+    def f():
         h_copy[1].wait_recv()
-        g_copy.wait_recv()
+        g_copy[0].wait_recv()
         q[first] = (tot[0, first] + e_in[3].astype(F32) + h_in[1].astype(F32) + g_in[...].astype(F32)).astype(BF16)
-    for k in range(2):
-        with jax.named_scope(f"last{k}"):
-            a_copy[0, k].wait_recv()
-            value = tot[0, rest[k]] + a_in[0, spans[k]].astype(F32)
-            for t in (2, 1) if k else (3, 2, 1):
-                b_copy[t, k].wait_recv()
-                value = value + b_in[t, spans[k]].astype(F32)
-            q[rest[k]] = value.astype(BF16)
+
+    def q_(k):
+        a_copy[0, k].wait_recv()
+        value = tot[0, rest[k]] + a_in[0, spans[k]].astype(F32)
+        for at in (2, 1) if k else (3, 2, 1):
+            b_copy[at, k].wait_recv()
+            value = value + b_in[at, spans[k]].astype(F32)
+        q[rest[k]] = value.astype(BF16)
+
+    steps = dict(o=o, t=t, s=s, p=p, h=h, g=g, f=f, q=q_)
+    for word in order:
+        with jax.named_scope("r" + word):
+            steps[word[0]](*map(int, word[1:]))
 
 
 def step_kernel(n, rate, flag, x_ref, g_ref, w_hbm, ls_hbm, rs_hbm, lr_hbm, rr_hbm,
@@ -396,10 +381,15 @@
         landed(fs.at[pl.ds(0, n // 2 - 1)], s_r.at[0])
         landed(us, u_r.at[0])
 
-    reduce_phase(
-        copies, f, fs, u, us, arrive, q, tot, keep,
-        a_out, a_in, b_out, b_in, e_out, e_in, h_out, h_in, g_out, g_in, a_r, b_r, e_r,
-    )
+    def reduce_in(order):
+        reduce_phase(
+            order, copies, f, fs, u, us, arrive, q, tot, keep,
+            a_out, a_in, b_out, b_in, e_out, e_in, h_out, h_in, g_out, g_in, a_r, b_r, e_r,
+        )
+
+    low = lax.div(me, LINE) < LINE // 2
+    pl.when(low)(functools.partial(reduce_in, LOW))
+    pl.when(jnp.logical_not(low))(functools.partial(reduce_in, HIGH))
     with jax.named_scope("drain"):
         q_out = pltpu.make_async_copy(q, q_ref, out_sem.at[5])
         q_out.start()

time: 64.7 us -> 63.7 us (0.985)
  Pallas kernels: 63.3 us -> 62.1 us
    pallas_call x1, Pallas kernels: 60.9 us -> 59.7 us  [fused_step(): pl.pallas_call(functools.partial(step_kernel, n, rate), out_shape=[jax.Sh...]
where the time goes in v5:
time: 63.7 us; the launch traced here: 63.4 us
  Pallas kernels  62.1 us (97%)
  between operations  1.29 us (2%)
    pallas_call x1, Pallas kernels, fused_step(): pl.pallas_call(functools.partial(step_kernel, n, rate), out_shape=[jax.Sh...  59.7 us
    pallas_call x1, Pallas kernels, hand_out(): pl.pallas_call(hand_out_kernel, out_shape=[jax.ShapeDtypeStruct(a.shape,...  2.41 us

profile of v5, /device:TPU:0, one launch (start us, length us, event | category | flops | bytes accessed | tf_op | source)
XLA Modules:
  0.0 63.4 jit_solution(8955055893537918840)
XLA Ops:
  1.3 59.7 %fused_step.1 = (f32[1,512,512]{2,1,0:T(8,128)S(1)}, f32[1,512,512]{2,1,0:T(8,128)S(1)}, f32[1,512,512]{2,1,0:T(8,128)S(1)}, f32[1,512,512]{2,1,0:T(8,128)S(1)},...) custom-call(s32[1]{0:T(128)S(6)} %copy.14.flag, bf16[128,8192]{1,0:T(8,128)(2,1)} %x_ref.1, ...), custom_call_target="tpu_custom_call" | custom-call | tf_op jit(solution)/shard_map/fused_step/pallas_call | solution.py:413
  61.0 2.4 %hand_out.1 = (f32[1,512,512]{2,1,0:T(8,128)}, f32[1,512,512]{2,1,0:T(8,128)}, f32[1,512,512]{2,1,0:T(8,128)}, f32[1,512,512]{2,1,0:T(8,128)}, f32[1,512,512]{2,1,0:T(8,128)}, /*index=5*/bf16[128,512]{1,0:T(8,128)(2,1)}) custom-call(f32[1,512,512]{2,1,0:T(8,128)S(1)} %get-tuple-element.12.refs_0_, f32[1,512,512]{2,1,0:T(8,128)S(1)} %get-tuple-element.13.refs_1_, ...), custom_call_target="tpu_custom_call" | custom-call | tf_op jit(solution)/shard_map/hand_out/pallas_call | solution.py:441

commit v6 on v5

--- a/solution.py
+++ b/solution.py
@@ -113,13 +113,15 @@
     pltpu.make_async_copy(view, view, sem).wait()
 
 
+SPANS = 3
+DIRECT = (0,)
 HIGH = (
-    "o3", "s3", "o1", "t3", "o2", "s2", "t1", "o0", "p30", "t2", "p31", "h", "s1", "s0", "t0",
-    "p20", "p21", "g", "p10", "p11", "f", "q0", "q1",
+    "o3", "s3", "o1", "t3", "o2", "s2", "t1", "o0", "p30", "t2", "p31", "p32", "h", "s1", "s0", "t0",
+    "p20", "p21", "p22", "g", "p10", "p11", "p12", "f", "q0", "q1", "q2",
 )
 LOW = (
-    "o1", "s1", "o3", "s3", "t1", "o2", "t3", "o0", "p10", "t2", "p11", "h", "s2", "s0", "t0",
-    "p30", "p31", "g", "p20", "p21", "f", "q0", "q1",
+    "o1", "s1", "o3", "s3", "t1", "o2", "t3", "o0", "p10", "t2", "p11", "p12", "s2", "h", "s0", "t0",
+    "p30", "p31", "p32", "p20", "p21", "p22", "g", "f", "q0", "q1", "q2",
 )
 
 
@@ -228,17 +230,17 @@
     return own_in[2]
 
 
-def reduce_phase(order, copies, feats, fs, u, us, arrive, q, tot, keep, a_out, a_in, b_out, b_in, e_out, e_in, h_out, h_in, g_out, g_in,
+def reduce_phase(order, copies, feats, fs, u, us, arrive, q, tot, ahead, keep, a_out, a_in, b_out, b_in, e_out, e_in, h_out, h_in, g_out, g_in,
                  a_r, b_r, e_r):
     me, mine = lax.axis_index("dp"), lax.axis_index("owner")
     row = flip(me, 2)
     rows = q.shape[0]
     cut = rows // 4
-    half = (rows - cut) // 2
+    third = (rows - cut) // SPANS
     go = copies.group(3)
     first = pl.ds(0, cut)
-    rest = [pl.ds(cut + k * half, half) for k in range(2)]
-    spans = [pl.ds(k * half, half) for k in range(2)]
+    rest = [pl.ds(cut + k * third, third) for k in range(SPANS)]
+    spans = [pl.ds(k * third, third) for k in range(SPANS)]
     near_z, far_z, direct, across = (toggle(me, LINE), mine), (toggle(me, 2 * LINE), mine), (toggle(me, 3 * LINE), mine), (row, mine)
 
     def near_part(base, t):
@@ -248,13 +250,13 @@
         return dot(fs[lax.div(toggle(base, LINE * t), 2)], us[...])
 
     a_copy, b_copy, h_copy, g_copy = {}, {}, [], []
-    lead = int(order[0][1])
-    ahead = near_part(row, lead)
+    for t in range(LINE):
+        ahead[t] = near_part(row, t)
     with jax.named_scope("swap"):
         arrive()
 
     def o(t):
-        value = (ahead if t == lead else near_part(row, t)) + far_part(row, t)
+        value = ahead[t] + far_part(row, t)
         a_out[t] = value[cut:].astype(BF16)
         if t % 2:
             early(0 if t == 3 else 1, value)
@@ -272,8 +274,8 @@
         go(e_out.at[k], e_in.at[k], e_r.at[k // 2], near_z)
 
     def s(t):
-        for k in range(2):
-            a_copy[t, k] = go(a_out.at[t, spans[k]], a_in.at[t, spans[k]], a_r.at[2 * t + k], across)
+        for k in range(SPANS):
+            a_copy[t, k] = go(a_out.at[t, spans[k]], a_in.at[t, spans[k]], a_r.at[SPANS * t + k], across)
 
     def p(t, k):
         a_copy[t, k].wait_recv()
@@ -281,13 +283,13 @@
         peer = near_z
         if t == 2:
             peer = far_z
-            if k:
+            if k not in DIRECT:
                 b_copy[3, k].wait_recv()
                 value = value + b_in[3, spans[k]].astype(F32)
-        elif (t, k) == (3, 0):
+        elif t == 3 and k in DIRECT:
             peer = direct
         b_out[t, spans[k]] = value.astype(BF16)
-        b_copy[t, k] = go(b_out.at[t, spans[k]], b_in.at[t, spans[k]], b_r.at[2 * t + k], peer)
+        b_copy[t, k] = go(b_out.at[t, spans[k]], b_in.at[t, spans[k]], b_r.at[SPANS * t + k], peer)
 
     def h():
         landed(e_in.at[pl.ds(0, 2)], e_r.at[0])
@@ -309,7 +311,7 @@
     def q_(k):
         a_copy[0, k].wait_recv()
         value = tot[0, rest[k]] + a_in[0, spans[k]].astype(F32)
-        for at in (2, 1) if k else (3, 2, 1):
+        for at in (3, 2, 1) if k in DIRECT else (2, 1):
             b_copy[at, k].wait_recv()
             value = value + b_in[at, spans[k]].astype(F32)
         q[rest[k]] = value.astype(BF16)
@@ -322,7 +324,7 @@
 
 def step_kernel(n, rate, flag, x_ref, g_ref, w_hbm, ls_hbm, rs_hbm, lr_hbm, rr_hbm,
                 ls_out, rs_out, lr_out, rr_out, d_out, q_ref,
-                f, fs, ga, grad, w, ls, rs, lr, rr, d, u, us, q, tot, keep, a_out, a_in, b_out, b_in, e_out, e_in, h_out, h_in, g_out, g_in,
+                f, fs, ga, grad, w, ls, rs, lr, rr, d, u, us, q, tot, ahead, keep, a_out, a_in, b_out, b_in, e_out, e_in, h_out, h_in, g_out, g_in,
                 in_sem, out_sem, send, own, x_r, p_r, z_r, y_r, c_r, s_r, u_r, a_r, b_r, e_r):
     me, mine = lax.axis_index("dp"), lax.axis_index("owner")
     pair = flip(me, 1)
@@ -383,7 +385,7 @@
 
     def reduce_in(order):
         reduce_phase(
-            order, copies, f, fs, u, us, arrive, q, tot, keep,
+            order, copies, f, fs, u, us, arrive, q, tot, ahead, keep,
             a_out, a_in, b_out, b_in, e_out, e_in, h_out, h_in, g_out, g_in, a_r, b_r, e_r,
         )
 
@@ -417,11 +419,11 @@
         out_specs=[anywhere] * 6,
         scratch_shapes=[
             pltpu.VMEM((n, rows, block), BF16), pltpu.VMEM((n // 2, rows, block), BF16), pltpu.VMEM((n, rows, width), BF16),
-        ] + [square] * 7 + [narrow] * 2 + [pltpu.VMEM((rows, width), BF16)] + [pltpu.VMEM((nz, rows, width), F32), pltpu.VMEM((2, cut, width), F32)] + [shards] * 4
+        ] + [square] * 7 + [narrow] * 2 + [pltpu.VMEM((rows, width), BF16)] + [pltpu.VMEM((nz, rows, width), F32)] * 2 + [pltpu.VMEM((2, cut, width), F32)] + [shards] * 4
         + [pltpu.VMEM((4, cut, width), BF16)] * 2 + [pltpu.VMEM((2, cut, width), BF16)] * 2 + [pltpu.VMEM((cut, width), BF16)] * 2
         + [dma((5,)), dma((6,)), dma((4,)), dma((3,))]
         + [dma((n + len(EXTRA) - 1,)), dma((n // 2,)), dma((LINE,)), dma((LINE,)), dma((2 * LINE,)), dma((1,)), dma((1,))]
-        + [dma((2 * LINE,)), dma((2 * LINE,)), dma((5,))],
+        + [dma((SPANS * LINE,)), dma((SPANS * LINE,)), dma((5,))],
         compiler_params=pltpu.CompilerParams(collective_id=0, has_side_effects=True, vmem_limit_bytes=48 << 20),
         name="fused_step",
     )(refresh, inputs, pltpu.with_memory_space_constraint(out_grads, pltpu.HBM), weights, left_stats, right_stats, left_roots, right_roots)
@@ -457,7 +459,7 @@
     col_blocks = col_count // block
     replicas = lax.axis_size("dp")
     tok_total = tok_local * replicas
-    kernels = col_blocks == 1 and lax.axis_size("owner") == 2 and replicas == 4 * LINE and block == 4 * tok_local
+    kernels = col_blocks == 1 and row_blocks == replicas == 4 * LINE and lax.axis_size("owner") == 2 and block == 4 * tok_local
     rate = 0.25 / math.sqrt(model_width)
     if kernels:
         return hand_out(*fused_step(

time: 63.7 us -> 63.4 us (level)
  no operation moved by 1% of the time
where the time goes in v6:
time: 63.4 us; the launch traced here: 63.3 us
  Pallas kernels  62 us (98%)
  between operations  1.29 us (2%)
    pallas_call x1, Pallas kernels, fused_step(): pl.pallas_call(functools.partial(step_kernel, n, rate), out_shape=[jax.Sh...  59.6 us
    pallas_call x1, Pallas kernels, hand_out(): pl.pallas_call(hand_out_kernel, out_shape=[jax.ShapeDtypeStruct(a.shape,...  2.41 us

profile of v6, /device:TPU:0, one launch (start us, length us, event | category | flops | bytes accessed | tf_op | source)
XLA Modules:
  0.0 63.3 jit_solution(3910538245392337702)
XLA Ops:
  1.3 59.6 %fused_step.1 = (f32[1,512,512]{2,1,0:T(8,128)S(1)}, f32[1,512,512]{2,1,0:T(8,128)S(1)}, f32[1,512,512]{2,1,0:T(8,128)S(1)}, f32[1,512,512]{2,1,0:T(8,128)S(1)},...) custom-call(s32[1]{0:T(128)S(6)} %copy.14.flag, bf16[128,8192]{1,0:T(8,128)(2,1)} %x_ref.1, ...), custom_call_target="tpu_custom_call" | custom-call | tf_op jit(solution)/shard_map/fused_step/pallas_call | solution.py:415
  60.8 2.4 %hand_out.1 = (f32[1,512,512]{2,1,0:T(8,128)}, f32[1,512,512]{2,1,0:T(8,128)}, f32[1,512,512]{2,1,0:T(8,128)}, f32[1,512,512]{2,1,0:T(8,128)}, f32[1,512,512]{2,1,0:T(8,128)}, /*index=5*/bf16[128,512]{1,0:T(8,128)(2,1)}) custom-call(f32[1,512,512]{2,1,0:T(8,128)S(1)} %get-tuple-element.12.refs_0_, f32[1,512,512]{2,1,0:T(8,128)S(1)} %get-tuple-element.13.refs_1_, ...), custom_call_target="tpu_custom_call" | custom-call | tf_op jit(solution)/shard_map/hand_out/pallas_call | solution.py:443
